TPU v7x, 128 devices: a whole 4x4x4 slice. The times are simulated.
128 devices in a mesh: outer: 8 (over x, core), inner: 16 (over z, y).
Axes of the slice: x: 4, y: 4, z: 4, core: 2. Of those that a mesh axis runs over, the one named last changes fastest.
Arguments:
- inputs: bfloat16 [512, 16, 16, 512], P(('outer', 'inner')), may hold values from -12 to 12
- cotangent: bfloat16 [512, 16, 16, 2048], P(('outer', 'inner')), may hold values from -12 to 12
- conv_weight: bfloat16 [4608, 512], replicated, may hold values from -1 to 1
- expand_weight: bfloat16 [512, 2048], replicated, may hold values from -2 to 2
- conv_momentum: float32 [128, 18432], P(('outer', 'inner')), may hold values from -6 to 6
- expand_momentum: float32 [128, 8192], P(('outer', 'inner')), may hold values from -6 to 6
Outputs:
- input_grad: bfloat16 [512, 16, 16, 512], P(('outer', 'inner'))
- conv_new: float32 [128, 18432], P(('outer', 'inner'))
- expand_new: float32 [128, 8192], P(('outer', 'inner'))
All inputs are finite; a program needn't handle non-finite values.
Results may differ from a plain program's by a relative error of at most 0.01.
Values may be sent and summed in bfloat16 or wider, within the bound.
A program may use at most 128 MiB of HBM per device.

v0:
```python
import jax
import jax.numpy as jnp
from jax import lax
from jax.sharding import PartitionSpec as P

EPS = 1e-06
MOMENTUM = 0.9


def from_partner(block, axis, stride):
    count = lax.axis_size(axis)
    route = []
    for low in range(count):
        high = low | 1 << stride
        if high != low and high < count:
            route += [(low, high), (high, low)]
    return lax.ppermute(block, axis, route)


def sent_to_all(x, axis):
    length = lax.axis_size(axis)
    return lax.all_to_all(jnp.broadcast_to(x[None], (length, *x.shape)), axis, 0, 0, tiled=True)


def of_everyone(x, axis):
    everything = sent_to_all(x, axis)
    return jnp.sum(everything, axis=0)


def patches(image):
    images, height, across, channels = image.shape
    padded = jnp.pad(image, ((0, 0), (1, 1), (1, 1), (0, 0)))
    pieces = [
        padded[:, shift_y : shift_y + height, shift_x : shift_x + across, :]
        for shift_y in range(3)
        for shift_x in range(3)
    ]
    return jnp.concatenate(pieces, axis=-1).reshape(images * height * across, 9 * channels)


def local_step(inputs, cotangent, conv_weight, expand_weight):
    images, height, across, channels = inputs.shape
    row_count = images * height * across
    relu_in = jnp.maximum(inputs, jnp.zeros((), inputs.dtype))
    columns = patches(relu_in)
    hidden_pre = jnp.dot(columns, conv_weight, preferred_element_type=jnp.float32).astype(
        jnp.bfloat16
    )
    hidden_act = jnp.maximum(hidden_pre, jnp.zeros((), hidden_pre.dtype))
    grad_rows = cotangent.reshape(row_count, cotangent.shape[-1])
    expand_grad = (
        lax.dot_general(
            hidden_act, grad_rows, (((0,), (0,)), ((), ())), preferred_element_type=jnp.float32
        )
        / row_count
    ).astype(jnp.bfloat16)
    hidden_back = lax.dot_general(
        grad_rows, expand_weight, (((1,), (1,)), ((), ())), preferred_element_type=jnp.float32
    )
    hidden_grad = jnp.where(hidden_pre > 0, hidden_back, 0.0).astype(jnp.bfloat16)
    conv_grad = (
        lax.dot_general(
            hidden_grad, columns, (((0,), (0,)), ((), ())), preferred_element_type=jnp.float32
        )
        / row_count
    ).astype(jnp.bfloat16)
    flipped = (
        conv_weight.reshape(3, 3, channels, channels)[::-1, ::-1]
        .transpose(0, 1, 3, 2)
        .reshape(9 * channels, channels)
    )
    back_cols = patches(hidden_grad.reshape(images, height, across, channels))
    input_back = jnp.dot(back_cols, flipped, preferred_element_type=jnp.float32)
    input_grad = jnp.where(inputs.reshape(row_count, channels) > 0, input_back, 0.0).astype(
        jnp.bfloat16
    )
    return (input_grad.reshape(inputs.shape), conv_grad, expand_grad)


def layer_stats(first, second, conv_len):
    conv_first = first[:, :conv_len]
    conv_second = second[:, :conv_len]
    expand_first = first[:, conv_len:]
    expand_second = second[:, conv_len:]
    return jnp.stack(
        [
            jnp.sum(conv_first * conv_first),
            jnp.sum(conv_second * conv_second),
            jnp.sum(conv_first * conv_second),
            jnp.sum(expand_first * expand_first),
            jnp.sum(expand_second * expand_second),
            jnp.sum(expand_first * expand_second),
        ]
    )


def coef_rows(stats, conv_len, expand_len):
    first_conv = 1.0 - stats[2] / (2.0 * (stats[0] + EPS))
    second_conv = 1.0 - stats[2] / (2.0 * (stats[1] + EPS))
    first_expand = 1.0 - stats[5] / (2.0 * (stats[3] + EPS))
    second_expand = 1.0 - stats[5] / (2.0 * (stats[4] + EPS))
    first_row = jnp.concatenate(
        [
            jnp.full((conv_len,), first_conv, jnp.float32),
            jnp.full((expand_len,), first_expand, jnp.float32),
        ]
    )
    second_row = jnp.concatenate(
        [
            jnp.full((conv_len,), second_conv, jnp.float32),
            jnp.full((expand_len,), second_expand, jnp.float32),
        ]
    )
    return (first_row, second_row)


def body(inputs, cotangent, conv_weight, expand_weight, conv_momentum, expand_momentum):
    input_grad, conv_grad, expand_grad = local_step(inputs, cotangent, conv_weight, expand_weight)
    outer_count = lax.axis_size("outer")
    inner_count = lax.axis_size("inner")
    conv_len = conv_momentum.shape[1]
    expand_len = expand_momentum.shape[1]
    conv_parts = conv_grad.astype(jnp.float32).reshape(outer_count, inner_count, conv_len)
    expand_parts = expand_grad.astype(jnp.float32).reshape(outer_count, inner_count, expand_len)
    joined = jnp.concatenate([conv_parts, expand_parts], axis=2)
    summed = lax.psum_scatter(
        joined.astype(jnp.bfloat16), "inner", scatter_dimension=1, tiled=True
    ).astype(jnp.float32)
    total_len = conv_len + expand_len
    holding = summed.reshape(outer_count, total_len)
    outer_pos = lax.axis_index("outer")
    levels = outer_count.bit_length() - 1
    for step_bit in range(levels):
        partner = from_partner(holding.astype(jnp.bfloat16), "outer", step_bit).astype(
            holding.dtype
        )
        stats = of_everyone(layer_stats(holding, partner, conv_len), "inner")
        mine_coef, partner_coef = coef_rows(stats, conv_len, expand_len)
        holding = mine_coef * holding + partner_coef * partner
    final = lax.dynamic_slice_in_dim(holding, outer_pos, 1, 0)
    conv_new = MOMENTUM * conv_momentum + final[:, :conv_len]
    expand_new = MOMENTUM * expand_momentum + final[:, conv_len:]
    return (input_grad, conv_new, expand_new)


def solution(mesh):
    return jax.shard_map(
        body,
        mesh=mesh,
        in_specs=(
            P(("outer", "inner"), None, None, None),
            P(("outer", "inner"), None, None, None),
            P(),
            P(),
            P(("outer", "inner"), None),
            P(("outer", "inner"), None),
        ),
        out_specs=(
            P(("outer", "inner"), None, None, None),
            P(("outer", "inner"), None),
            P(("outer", "inner"), None),
        ),
        check_vma=False,
    )
```

profile of v0, /device:TPU:1, one launch (start us, length us, event | category | flops | bytes accessed | tf_op | source)
XLA Modules:
  0.0 251.0 jit_solution(7718275045800611092)
XLA Ops:
  7.2 1.5 broadcast_maximum_fusion
  11.4 5.0 %convolution_convert_fusion = bf16[1024,512]{1,0:T(8,128)(2,1)S(1)} fusion(bf16[1024,4608]{1,0:T(8,128)(2,1)S(1)} %bitcast.78, bf16[4608,512]{1,0:T(8,128)(2,1)S(1)} %bitcast.63), kind=kOutput, calls=%fused_computation.22 | convolution fusion | flops 4832362496 | bytes 15204352 | tf_op jit(solution)/shard_map/dot_general | solution.py:46
  16.4 3.7 %multiply_convert_fusion.1 = bf16[512,2048]{1,0:T(8,128)(2,1)} fusion(bf16[1024,2048]{1,0:T(8,128)(2,1)S(1)} %bitcast.80, bf16[1024,512]{1,0:T(8,128)(2,1)S(1)} %convolution_convert_fusion), kind=kOutput, calls=%fused_computation.3 | convolution fusion | flops 2150105088 | bytes 7340032 | tf_op jit(solution)/shard_map/dot_general | solution.py:52
  20.1 2.4 select_convert_fusion.1
  22.5 1.0 copy-done.3
  23.4 7.0 %multiply_convert_fusion = bf16[512,4608]{1,0:T(8,128)(2,1)} fusion(bf16[1024,512]{1,0:T(8,128)(2,1)S(1)} %select_convert_fusion.1, bf16[1024,4608]{1,0:T(8,128)(2,1)S(1)} %bitcast.79), kind=kOutput, calls=%fused_computation | convolution fusion | flops 4836556800 | bytes 15204352 | tf_op jit(solution)/shard_map/dot_general | solution.py:62
  30.4 8.4 %reshape.166 = bf16[8,16,18432]{2,1,0:T(8,128)(2,1)} reshape(bf16[512,4608]{1,0:T(8,128)(2,1)} %multiply_convert_fusion) | data formatting | bytes 9437184 | tf_op jit(solution)/shard_map/reshape | solution.py:123
  38.8 7.1 %copy.29 = bf16[8,16,18432]{2,0,1:T(8,128)(2,1)} copy(bf16[8,16,18432]{2,1,0:T(8,128)(2,1)} %reshape.166) | data formatting | bytes 9437184 | tf_op jit(solution)/shard_map/reshape | solution.py:123
  45.9 3.4 %reshape.167 = bf16[8,16,8192]{2,1,0:T(8,128)(2,1)S(1)} reshape(bf16[512,2048]{1,0:T(8,128)(2,1)} %multiply_convert_fusion.1) | data formatting | bytes 4194304 | tf_op jit(solution)/shard_map/reshape | solution.py:124
  49.3 1.2 copy.30
  50.4 5.7 %pad_maximum_fusion = bf16[8,16,26624]{2,0,1:T(8,128)(2,1)} fusion(bf16[8,16,8192]{2,0,1:T(8,128)(2,1)S(1)} %copy.30, bf16[8,16,18432]{2,0,1:T(8,128)(2,1)} %copy.29), kind=kLoop, calls=%fused_computation.1 | loop fusion | flops 13631488 | bytes 13631488 | tf_op jit(solution)/shard_map/concatenate | solution.py:125
  56.2 6.6 %pad_slice_fusion = (bf16[4,16,16,512]{3,2,1,0:T(8,128)(2,1)S(1)}, bf16[4,16,16,512]{3,2,1,0:T(8,128)(2,1)S(1)}, bf16[4,16,16,512]{3,2,1,0:T(8,128)(2,1)S(1)}, b...) fusion(bf16[4,16,16,512]{3,2,1,0:T(8,128)(2,1)} %bitcast.72), kind=kLoop, calls=%fused_computation.4 | loop fusion | bytes 9437184 | tf_op jit(solution)/shard_map/slice | solution.py:34
  63.2 3.6 %copy-done.9 = bf16[1024,4608]{1,0:T(8,128)(2,1)} copy-done((bf16[1024,4608]{1,0:T(8,128)(2,1)}, bf16[1024,4608]{1,0:T(8,128)(2,1)S(1)}, u32[]{:S(2)}) %copy-start.9) | copy-done | bytes 9437208
  66.9 2.4 reverse_bitcast_fusion
  69.2 71.7 %reduce-scatter.4.cloned.1.call-done = bf16[8,1,26624]{2,0,1:T(8,128)(2,1)} async-done(((bf16[8,16,26624]{2,0,1:T(8,128)(2,1)}), bf16[8,1,26624]{2,0,1:T(8,128)(2,1)}) %reduce-scatter.4.cloned.1.call-update) | async-done | bytes 426000
  140.9 2.0 collective-permute-start
  142.9 1.1 bitcast_convert_fusion
  144.6 0.8 multiply_reduce_fusion.15
  145.4 0.9 multiply_reduce_fusion.6
  146.2 4.0 %stack.69 = f32[6]{0:T(128)S(1)} concatenate(f32[1]{0:T(128)} %bitcast.17, f32[1]{0:T(128)} %bitcast.18, f32[1]{0:T(128)} %bitcast.19, f32[1]{0:T(128)} %bitcast.20, f32[1]{0:T(128)} %bitcast.21, f32[1]{0:T(128)} %bitcast.22), dimensions={0} | concatenate | bytes 48 | tf_op jit(solution)/shard_map/stack | solution.py:85
  150.8 4.7 %all-to-all-start = ((f32[16,1,6]{2,1,0:T(1,128)}), f32[16,1,6]{2,1,0:T(1,128)S(1)}, u32[]{:S(2)}, u32[]{:S(2)}) async-start(f32[16,1,6]{2,1,0:T(1,128)} %broadcast_in_dim.24), calls=%async_computation | async-start | bytes 16384 | tf_op jit(solution)/shard_map/all_to_all | solution.py:22
  155.5 2.4 constant_dynamic-update-slice_fusion.4
  157.9 4.0 %all-to-all-done = f32[16,1,6]{2,1,0:T(1,128)S(1)} async-done(((f32[16,1,6]{2,1,0:T(1,128)}), f32[16,1,6]{2,1,0:T(1,128)S(1)}, u32[]{:S(2)}, u32[]{:S(2)}) %all-to-all-start) | async-done | bytes 416 | tf_op jit(solution)/shard_map/all_to_all | solution.py:22
  161.9 0.7 fusion.16
  167.8 1.3 fusion.13
  169.1 1.5 collective-permute-start.1
  170.6 2.3 constant_dynamic-update-slice_fusion.3
  172.8 2.3 constant_dynamic-update-slice_fusion.2
  175.1 1.1 broadcast_compare_fusion
  176.2 2.7 %collective-permute-done.1 = bf16[8,26624]{1,0:T(8,128)(2,1)S(1)} collective-permute-done((bf16[8,26624]{1,0:T(8,128)(2,1)S(1)}, bf16[8,26624]{1,0:T(8,128)(2,1)S(1)}, u32[]{:S(2)}, u32[]{:S(2)}) %collective-permute-start.1) | collective-permute-done | bytes 426016 | tf_op jit(solution)/shard_map/ppermute | solution.py:17
  179.0 0.8 multiply_reduce_fusion.12
  179.8 0.9 multiply_reduce_fusion.3
  180.7 4.1 %stack.76 = f32[6]{0:T(128)S(1)} concatenate(f32[1]{0:T(128)} %bitcast.27, f32[1]{0:T(128)} %bitcast.28, f32[1]{0:T(128)} %bitcast.29, f32[1]{0:T(128)} %bitcast.30, f32[1]{0:T(128)} %bitcast.31, f32[1]{0:T(128)} %bitcast.32), dimensions={0} | concatenate | bytes 48 | tf_op jit(solution)/shard_map/stack | solution.py:85
  185.4 3.5 %all-to-all-start.1 = ((f32[16,1,6]{2,1,0:T(1,128)}), f32[16,1,6]{2,1,0:T(1,128)S(1)}, u32[]{:S(2)}, u32[]{:S(2)}) async-start(f32[16,1,6]{2,1,0:T(1,128)} %broadcast_in_dim.27), calls=%async_computation.1 | async-start | bytes 16384 | tf_op jit(solution)/shard_map/all_to_all | solution.py:22
  188.8 1.1 constant_dynamic-update-slice_fusion.1
  189.9 6.6 %copy.28 = bf16[3,3,512,512]{3,2,1,0:T(8,128)(2,1)} copy(bf16[3,3,512,512]{2,3,1,0:T(8,128)(2,1)} %reverse_bitcast_fusion) | data formatting | bytes 9437184 | tf_op jit(solution)/shard_map/transpose | solution.py:69
  196.6 0.7 fusion.15
  202.7 0.9 fusion.12
  203.6 2.7 %collective-permute-start.2 = (bf16[8,26624]{1,0:T(8,128)(2,1)}, bf16[8,26624]{1,0:T(8,128)(2,1)S(1)}, u32[]{:S(2)}, u32[]{:S(2)}) collective-permute-start(bf16[8,26624]{1,0:T(8,128)(2,1)} %get-tuple-element.21), channel_id=1, source_target_pairs={{0,64},{64,0},{16,80},{80,16},{32,96},{96,32},{48,112},{112,48},{1... | collective-permute-start | bytes 1277960 | tf_op jit(solution)/shard_map/ppermute | solution.py:17
  206.3 10.0 %select_convert_fusion = bf16[1024,512]{1,0:T(8,128)(2,1)} fusion(pred[4,16,16,512]{3,2,1,0:T(8,128)(4,1)} %broadcast_compare_fusion, bf16[1024,4608]{1,0:T(8,128)(2,1)} %constant_dynamic-update-slice_fusion.1, bf16[4608,512]{1,0:T(8,128)(2,1)} %bitcast.67), kind=kOutput, calls=%fused_computation.20 | convolution fusion | flops 4832886784 | bytes 15728640 | tf_op jit(solution)/shard_map/dot_general | solution.py:73
  216.4 0.9 multiply_reduce_fusion.9
  217.3 0.9 multiply_reduce_fusion
  218.1 3.9 %stack.83 = f32[6]{0:T(128)S(1)} concatenate(f32[1]{0:T(128)} %bitcast.37, f32[1]{0:T(128)} %bitcast.38, f32[1]{0:T(128)} %bitcast.39, f32[1]{0:T(128)} %bitcast.40, f32[1]{0:T(128)} %bitcast.41, f32[1]{0:T(128)} %bitcast.42), dimensions={0} | concatenate | bytes 48 | tf_op jit(solution)/shard_map/stack | solution.py:85
  222.6 6.6 %all-to-all-start.2 = ((f32[16,1,6]{2,1,0:T(1,128)}), f32[16,1,6]{2,1,0:T(1,128)S(1)}, u32[]{:S(2)}, u32[]{:S(2)}) async-start(f32[16,1,6]{2,1,0:T(1,128)} %broadcast_in_dim.30), calls=%async_computation.2 | async-start | bytes 16384 | tf_op jit(solution)/shard_map/all_to_all | solution.py:22
  229.2 6.4 %all-to-all-done.2 = f32[16,1,6]{2,1,0:T(1,128)S(1)} async-done(((f32[16,1,6]{2,1,0:T(1,128)}), f32[16,1,6]{2,1,0:T(1,128)S(1)}, u32[]{:S(2)}, u32[]{:S(2)}) %all-to-all-start.2) | async-done | bytes 416 | tf_op jit(solution)/shard_map/all_to_all | solution.py:22
  235.6 0.7 fusion.14
  241.3 1.4 fusion.10
  242.7 0.7 slice_add_fusion
  (75 shorter events, 6.4 us)
Async XLA Ops:
  7.2 12.9 %copy-start = (bf16[512,2048]{1,0:T(8,128)(2,1)S(1)}, bf16[512,2048]{1,0:T(8,128)(2,1)}, u32[]{:S(2)}) copy-start(bf16[512,2048]{1,0:T(8,128)(2,1)} %param.9) | copy-start | bytes 6291460
  7.2 2.7 %copy-start.2 = (bf16[4,16,16,512]{3,2,1,0:T(8,128)(2,1)S(1)}, bf16[4,16,16,512]{3,2,1,0:T(8,128)(2,1)}, u32[]{:S(2)}) copy-start(bf16[4,16,16,512]{3,2,1,0:T(8,128)(2,1)} %param.6) | copy-start | bytes 3145732
  7.2 133.8 %reduce-scatter.4.cloned.1.call-start = ((), (), s32[]{:S(2)}) async-start(), calls=%async_computation.4 | async-start | bytes 7241728
  8.7 2.6 %slice-start = ((s8[4718592]{0:T(1024)(128)(4,1)}), s8[4194304]{0:T(1024)(128)(4,1)S(1)}, s32[]{:S(2)}) async-start(s8[4718592]{0:T(1024)(128)(4,1)} %bitcast.62), calls=%async_computation.5 | async-start | bytes 8388608
  9.9 1.5 slice-start.1
  11.4 5.0 %copy-start.12 = (bf16[4,16,16,2048]{3,2,1,0:T(8,128)(2,1)S(1)}, bf16[4,16,16,2048]{3,2,1,0:T(8,128)(2,1)}, u32[]{:S(2)}) copy-start(bf16[4,16,16,2048]{3,2,1,0:T(8,128)(2,1)} %param.7) | copy-start | bytes 12582916
  22.5 1.0 copy-start.3
  56.2 7.0 %copy-start.4 = (bf16[1024,512]{1,0:T(8,128)(2,1)S(1)}, bf16[1024,512]{1,0:T(8,128)(2,1)}, u32[]{:S(2)}) copy-start(bf16[1024,512]{1,0:T(8,128)(2,1)} %copy-done.3) | copy-start | bytes 3145732
  56.2 10.7 %slice-start.2 = ((s8[4718592]{0:T(1024)(128)(4,1)}), s8[4194304]{0:T(1024)(128)(4,1)S(1)}, s32[]{:S(2)}) async-start(s8[4718592]{0:T(1024)(128)(4,1)} %bitcast.64), calls=%async_computation.7 | async-start | bytes 8388608
  62.8 4.0 %slice-start.3 = ((s8[4718592]{0:T(1024)(128)(4,1)}), s8[524288]{0:T(1024)(128)(4,1)S(1)}, s32[]{:S(2)}) async-start(s8[4718592]{0:T(1024)(128)(4,1)} %bitcast.64), calls=%async_computation.8 | async-start | bytes 1048576
  63.2 3.6 %copy-start.9 = (bf16[1024,4608]{1,0:T(8,128)(2,1)}, bf16[1024,4608]{1,0:T(8,128)(2,1)S(1)}, u32[]{:S(2)}) copy-start(bf16[1024,4608]{1,0:T(8,128)(2,1)S(1)} %constant_dynamic-update-slice_fusion.5) | copy-start | bytes 28311556
  140.9 3.6 %collective-permute-start = (bf16[8,26624]{1,0:T(8,128)(2,1)}, bf16[8,26624]{1,0:T(8,128)(2,1)S(1)}, u32[]{:S(2)}, u32[]{:S(2)}) collective-permute-start(bf16[8,26624]{1,0:T(8,128)(2,1)} %bitcast.77), channel_id=1, source_target_pairs={{0,16},{16,0},{32,48},{48,32},{64,80},{80,64},{96,112},{112,96},{1... | collective-permute-start | bytes 1277960 | tf_op jit(solution)/shard_map/ppermute | solution.py:17
  144.5 1.7 copy-start.6
  150.8 11.0 %all-to-all-start = ((f32[16,1,6]{2,1,0:T(1,128)}), f32[16,1,6]{2,1,0:T(1,128)S(1)}, u32[]{:S(2)}, u32[]{:S(2)}) async-start(f32[16,1,6]{2,1,0:T(1,128)} %broadcast_in_dim.24), calls=%async_computation | async-start | bytes 16384 | tf_op jit(solution)/shard_map/all_to_all | solution.py:22
  169.1 9.9 %collective-permute-start.1 = (bf16[8,26624]{1,0:T(8,128)(2,1)S(1)}, bf16[8,26624]{1,0:T(8,128)(2,1)S(1)}, u32[]{:S(2)}, u32[]{:S(2)}) collective-permute-start(bf16[8,26624]{1,0:T(8,128)(2,1)S(1)} %get-tuple-element.23), channel_id=1, source_target_pairs={{0,32},{32,0},{16,48},{48,16},{64,96},{96,64},{80,112},{112,80},{1... | collective-permute-start | bytes 1277960 | tf_op jit(solution)/shard_map/ppermute | solution.py:17
  178.9 1.7 copy-start.7
  180.7 22.0 %copy-start.8 = (bf16[8,26624]{1,0:T(8,128)(2,1)S(1)}, bf16[8,26624]{1,0:T(8,128)(2,1)}, u32[]{:S(2)}) copy-start(bf16[8,26624]{1,0:T(8,128)(2,1)} %copy-done.7) | copy-start | bytes 1277956
  185.4 11.2 %all-to-all-start.1 = ((f32[16,1,6]{2,1,0:T(1,128)}), f32[16,1,6]{2,1,0:T(1,128)S(1)}, u32[]{:S(2)}, u32[]{:S(2)}) async-start(f32[16,1,6]{2,1,0:T(1,128)} %broadcast_in_dim.27), calls=%async_computation.1 | async-start | bytes 16384 | tf_op jit(solution)/shard_map/all_to_all | solution.py:22
  203.6 12.7 %collective-permute-start.2 = (bf16[8,26624]{1,0:T(8,128)(2,1)}, bf16[8,26624]{1,0:T(8,128)(2,1)S(1)}, u32[]{:S(2)}, u32[]{:S(2)}) collective-permute-start(bf16[8,26624]{1,0:T(8,128)(2,1)} %get-tuple-element.21), channel_id=1, source_target_pairs={{0,64},{64,0},{16,80},{80,16},{32,96},{96,32},{48,112},{112,48},{1... | collective-permute-start | bytes 1277960 | tf_op jit(solution)/shard_map/ppermute | solution.py:17
  206.3 36.4 %copy-start.10 = (f32[1,18432]{1,0:T(1,128)S(1)}, f32[1,18432]{1,0:T(1,128)}, u32[]{:S(2)}) copy-start(f32[1,18432]{1,0:T(1,128)} %param.10) | copy-start | bytes 221188
  206.3 37.2 %copy-start.11 = (f32[1,8192]{1,0:T(1,128)S(1)}, f32[1,8192]{1,0:T(1,128)}, u32[]{:S(2)}) copy-start(f32[1,8192]{1,0:T(1,128)} %param.11) | copy-start | bytes 98308
  206.3 37.8 %copy-start.1 = (bf16[512,2048]{1,0:T(8,128)(2,1)S(1)}, bf16[512,2048]{1,0:T(8,128)(2,1)}, u32[]{:S(2)}) copy-start(bf16[512,2048]{1,0:T(8,128)(2,1)} %param.9) | copy-start | bytes 6291460
  216.4 0.9 copy-start.5
  222.6 13.0 %all-to-all-start.2 = ((f32[16,1,6]{2,1,0:T(1,128)}), f32[16,1,6]{2,1,0:T(1,128)S(1)}, u32[]{:S(2)}, u32[]{:S(2)}) async-start(f32[16,1,6]{2,1,0:T(1,128)} %broadcast_in_dim.30), calls=%async_computation.2 | async-start | bytes 16384 | tf_op jit(solution)/shard_map/all_to_all | solution.py:22
Sparse Core Ops, SparseCore 0:
  56.3 84.6 reduce-scatter.3
where the time goes:
time: 256 us; the launch traced here: 251 us
  waiting for transfers between devices  85.3 us (33%)
  local copies, waits for them, and re-layouts  66.8 us (26%)
  between operations  29.9 us (12%)
  matrix products  28 us (11%)
  starting transfers between devices  20.9 us (8%)
  other arithmetic  20 us (8%)
    unnamed x2, waiting for transfers between devices  71.7 us
    reshape x2, local copies, waits for them, and re-layouts, body(): conv_grad.astype(jnp.float32).reshape(outer_count, inner_count, conv_len)  15.5 us
    all_to_all x3, starting transfers between devices, sent_to_all(): lax.all_to_all(jnp.broadcast_to(x[None], (length, *x.shape)), axis, 0, 0,...  14.7 us
    unnamed x49, local copies, waits for them, and re-layouts  13.9 us
    another operation x3, local copies, waits for them, and re-layouts, layer_stats(): jnp.stack([jnp.sum(conv_first * conv_first), jnp.sum(conv_second * conv_s...  11.9 us
    all_to_all x3, waiting for transfers between devices, sent_to_all(): lax.all_to_all(jnp.broadcast_to(x[None], (length, *x.shape)), axis, 0, 0,...  10.3 us
    dot_general x1, matrix products, local_step(): input_back = jnp.dot(back_cols, flipped, preferred_element_type=jnp.float32)  10 us
    transpose x2, local copies, waits for them, and re-layouts, local_step(): flipped = conv_weight.reshape(3, 3, channels, channels)[::-1, ::-1].trans...  9.01 us
  transfers between devices with their start and end apart: 7, of which 5 were waited for; matrix products, arithmetic and copies ran while one was open for 14% of the time, Pallas kernels for 0%

commit v1 on v0

v1 whole, which is shorter than its diff:
```python
import jax
import jax.numpy as jnp
from jax import lax
from jax.experimental import pallas as pl
from jax.experimental.pallas import tpu as pltpu
from jax.sharding import PartitionSpec as P

EPS = 1e-06
MOMENTUM = 0.9
F32 = jnp.float32
BF16 = jnp.bfloat16
MESH = pl.DeviceIdType.MESH

PAIRS = 13
LAG2, LAG3, LAG4, LAG5, LAG6 = 1, 3, 4, 5, 7
GRAM = [(a, b) for a in range(8) for b in range(a, 8)]
GRAM_AT = {ab: n for n, ab in enumerate(GRAM)}


def nn(a, b):
    return lax.dot_general(a, b, (((1,), (0,)), ((), ())), preferred_element_type=F32)


def nt(a, b):
    return lax.dot_general(a, b, (((1,), (1,)), ((), ())), preferred_element_type=F32)


def adasum_weights(gram):
    count = 8
    weights = [None] * 8
    span = 1
    while count > 1:
        coefs = []
        for m in range(count // 2):
            a, b = 2 * m, 2 * m + 1
            dot = gram[(a, b)]
            coefs.append(
                (
                    1.0 - dot / (2.0 * (gram[(a, a)] + EPS)),
                    1.0 - dot / (2.0 * (gram[(b, b)] + EPS)),
                )
            )
        merged = {}
        for m in range(count // 2):
            for n in range(m, count // 2):
                total = None
                for s in range(2):
                    for t in range(2):
                        key = (min(2 * m + s, 2 * n + t), max(2 * m + s, 2 * n + t))
                        term = coefs[m][s] * coefs[n][t] * gram[key]
                        total = term if total is None else total + term
                merged[(m, n)] = jnp.maximum(total, 0.0) if m == n else total
        for o in range(8):
            group = o // span
            c = coefs[group // 2][group % 2]
            weights[o] = c if weights[o] is None else weights[o] * c
        gram = merged
        count //= 2
        span *= 2
    return weights


def kernel(
    x_hbm, cot_hbm, w_hbm, we_hbm,
    ig_hbm, fin_conv, fin_exp,
    xin, xs, wt, we, cot, acc, hp, ht, hg, hs, acc2, perm,
    gm, r1p, r1m, r2p, r2m, tb, r3p, r3m, r4p, r4m, ub, rx, gacc, stat, st1, st2,
    in_sem, w_sem, we_sem, cot_sem, out_sem,
    q1p, q1m, q2p, q2m, q3p, q3m, q4p, q4m, qx, qs1, qs2,
    s1p, s1m, s2p, s2m, s3p, s3m, s4p, s4m, sx, ss1, ss2,
):
    o = lax.axis_index("outer")
    i = lax.axis_index("inner")
    z = i // 4
    y = i % 4

    barrier = pltpu.get_barrier_semaphore()

    def greet_outer(d, carry):
        pl.semaphore_signal(barrier, inc=1, device_id={"outer": (o + d) % 8}, device_id_type=MESH)
        return carry

    def greet_inner(d, carry):
        pl.semaphore_signal(barrier, inc=1, device_id={"inner": (i + d) % 16}, device_id_type=MESH)
        return carry

    lax.fori_loop(1, 8, greet_outer, 0)
    lax.fori_loop(1, 16, greet_inner, 0)

    def w_copy(h, t):
        return pltpu.make_async_copy(
            w_hbm.at[pl.ds(pl.multiple_of(t * 512, 512), 512), pl.ds(pl.multiple_of(h * 256, 256), 256)],
            wt.at[h, t],
            w_sem.at[h, t],
        )

    def cot_copy(j):
        return pltpu.make_async_copy(cot_hbm.at[:, pl.ds(j * 512, 512)], cot.at[j], cot_sem.at[j])

    def we_copy(j):
        return pltpu.make_async_copy(we_hbm.at[:, pl.ds(j * 512, 512)], we.at[j], we_sem.at[j])

    in_copy = pltpu.make_async_copy(x_hbm, xin, in_sem)
    in_copy.start()

    def start_w(h):
        def one(t, carry):
            w_copy(h, t).start()
            return carry

        lax.fori_loop(0, 9, one, 0)

    start_w(0)
    for j in range(4):
        cot_copy(j).start()
    for j in range(4):
        we_copy(j).start()
    start_w(1)

    row = lax.broadcasted_iota(jnp.int32, (256, 256), 0)
    col = lax.broadcasted_iota(jnp.int32, (256, 256), 1)
    want = ((row // 4) % 4) * 64 + (row // 16) * 4 + row % 4
    perm[...] = jnp.where(want == col, 1.0, 0.0).astype(BF16)

    zero_row = jnp.zeros((16, 512), BF16)
    for dst in (xs, hs):
        for dx in range(3):
            for b in range(4):
                dst[dx, b, 0] = zero_row
                dst[dx, b, 17] = zero_row
    gacc[...] = jnp.zeros_like(gacc)

    def spread(value, dst, b, r, lanes):
        n = value.shape[1]
        w = lax.broadcasted_iota(jnp.int32, (64, n), 0) % 16
        wide = value.astype(F32)
        left = jnp.where(w == 0, 0.0, pltpu.roll(wide, 1, 0)).astype(BF16)
        right = jnp.where(w == 15, 0.0, pltpu.roll(wide, 63, 0)).astype(BF16)
        for dx, v in ((0, left), (1, value), (2, right)):
            dst[dx, b, pl.ds(1 + 4 * r, 4), :, lanes] = v.reshape(4, 16, n)

    in_copy.wait()

    def prep(g, carry):
        b, r = g // 4, g % 4
        v = xin[b, pl.ds(4 * r, 4)].reshape(64, 512)
        spread(jnp.maximum(v, jnp.zeros((), BF16)), xs, b, r, slice(None))
        return carry

    lax.fori_loop(0, 16, prep, 0)

    def tap(ref, t):
        return ref[t % 3, :, pl.ds(t // 3, 16)].reshape(1024, 512)

    def conv_taps(h, first, last):
        def one(t, carry):
            w_copy(h, t).wait()
            part = nn(tap(xs, t), wt[h, t])

            @pl.when(t == 0)
            def _():
                acc[...] = part

            @pl.when(t > 0)
            def _():
                acc[...] += part

            return carry

        lax.fori_loop(first, last, one, 0)

    def finish_forward(h):
        pre = acc[...].astype(BF16)
        hp[h] = pre
        ht[0, h] = nt(perm[...], jnp.maximum(pre, jnp.zeros((), BF16))).astype(BF16)

    def hidden_back(h, first, last):
        def one(k, carry):
            rows = pl.ds(pl.multiple_of(k * 256, 256), 256)
            chans = pl.ds(pl.multiple_of(h * 256, 256), 256)
            back = nt(cot[0, rows], we[0, chans])
            for j in range(1, 4):
                back = back + nt(cot[j, rows], we[j, chans])
            hg[h, rows] = jnp.where(hp[h, rows].astype(F32) > 0, back, 0.0).astype(BF16)
            return carry

        lax.fori_loop(first, last, one, 0)

    def finish_back(h):
        ht[1, h] = nt(perm[...], hg[h]).astype(BF16)

    def produce(p, k):
        q = 2 * p + k
        h = q // 13
        j = q % 13

        @pl.when(j < 4)
        def _():
            g = nn(ht[0, h], cot[j]) * (1.0 / 1024.0)
            gm[q] = g.astype(BF16).reshape(4, 4, 16, 512)

        @pl.when(j >= 4)
        def _():
            g = nn(ht[1, h], tap(xs, j - 4)) * (1.0 / 1024.0)
            gm[q] = g.astype(BF16).reshape(4, 4, 16, 512)

    def ring(k, stage):
        if (k + stage) % 2 == 0:
            return z, ((z + 1) % 4) * 4 + y, ((z + 3) % 4) * 4 + y
        return y, z * 4 + (y + 1) % 4, z * 4 + (y + 3) % 4

    def block(p, k, at):
        q = 2 * p + k
        return gm.at[q, at] if k == 0 else gm.at[q, :, at]

    def remote(src, dst, send, recv, inner):
        return pltpu.make_async_remote_copy(
            src_ref=src, dst_ref=dst, send_sem=send, recv_sem=recv,
            device_id={"inner": inner}, device_id_type=MESH,
        )

    LO, HI = slice(0, 256), slice(256, 512)

    def copies1(p, k):
        at, nxt, prv = ring(k, 0)
        far = block(p, k, (at + 2) % 4)
        return (
            remote(far.at[:, :, LO], r1p.at[p, k], s1p, q1p.at[p, k], nxt),
            remote(far.at[:, :, HI], r1m.at[p, k], s1m, q1m.at[p, k], prv),
        )

    def copies2(p, k):
        at, nxt, prv = ring(k, 0)
        return (
            remote(block(p, k, (at + 1) % 4), r2p.at[p, k], s2p, q2p.at[p, k], nxt),
            remote(block(p, k, (at + 3) % 4), r2m.at[p, k], s2m, q2m.at[p, k], prv),
        )

    def copies3(p, k):
        at, nxt, prv = ring(k, 1)
        far = tb.at[p, k, (at + 2) % 4]
        return (
            remote(far.at[:, LO], r3p.at[p, k], s3p, q3p.at[p, k], nxt),
            remote(far.at[:, HI], r3m.at[p, k], s3m, q3m.at[p, k], prv),
        )

    def copies4(p, k):
        at, nxt, prv = ring(k, 1)
        return (
            remote(tb.at[p, k, (at + 1) % 4], r4p.at[p, k], s4p, q4p.at[p, k], nxt),
            remote(tb.at[p, k, (at + 3) % 4], r4m.at[p, k], s4m, q4m.at[p, k], prv),
        )

    def step1(p, k):
        for c in copies1(p, k):
            c.start()

    def step2(p, k):
        at, _, _ = ring(k, 0)
        fwd, bwd = copies1(p, k)
        out_fwd, out_bwd = copies2(p, k)
        near = block(p, k, (at + 1) % 4)
        fwd.wait_recv()
        near[:, :, LO] = (near[:, :, LO].astype(F32) + r1p[p, k].astype(F32)).astype(BF16)
        out_fwd.start()
        near = block(p, k, (at + 3) % 4)
        bwd.wait_recv()
        near[:, :, HI] = (near[:, :, HI].astype(F32) + r1m[p, k].astype(F32)).astype(BF16)
        out_bwd.start()

    def step3(p, k):
        at, _, _ = ring(k, 0)
        for c in copies2(p, k):
            c.wait_recv()
        mine = block(p, k, at)
        total = mine[...].astype(F32) + r2p[p, k].astype(F32) + r2m[p, k].astype(F32)
        tb[p, k] = total.astype(BF16)
        for c in copies3(p, k):
            c.start()

    def step4(p, k):
        at, _, _ = ring(k, 1)
        fwd, bwd = copies3(p, k)
        out_fwd, out_bwd = copies4(p, k)
        near = tb.at[p, k, (at + 1) % 4]
        fwd.wait_recv()
        near[:, LO] = (near[:, LO].astype(F32) + r3p[p, k].astype(F32)).astype(BF16)
        out_fwd.start()
        near = tb.at[p, k, (at + 3) % 4]
        bwd.wait_recv()
        near[:, HI] = (near[:, HI].astype(F32) + r3m[p, k].astype(F32)).astype(BF16)
        out_bwd.start()

    def x_copy(p, k, part, j, dest):
        return pltpu.make_async_remote_copy(
            src_ref=ub.at[p, k, part], dst_ref=rx.at[j, o], send_sem=sx, recv_sem=qx.at[j],
            device_id={"outer": dest}, device_id_type=MESH,
        )

    def step5(p, k):
        at, _, _ = ring(k, 1)
        q = 2 * p + k
        h = q // 13
        j = q % 13
        for c in copies4(p, k):
            c.wait_recv()
        total = tb[p, k, at].astype(F32) + r4p[p, k].astype(F32) + r4m[p, k].astype(F32)
        for part in range(4):
            dest = h * 4 + part
            ub[p, k, part] = total[4 * part : 4 * part + 4]

            @pl.when(dest != o)
            def _():
                x_copy(p, k, part, j, dest).start()

            @pl.when(dest == o)
            def _():
                rx[j, o] = total[4 * part : 4 * part + 4]

    def step6(p, k):
        q = 2 * p + k
        j = q % 13

        @pl.when(q // 13 == o // 4)
        def _():
            pltpu.make_async_remote_copy(
                src_ref=rx.at[j, pl.ds(0, 7)], dst_ref=rx.at[j, pl.ds(0, 7)], send_sem=sx, recv_sem=qx.at[j],
                device_id={"outer": (o + 1) % 8}, device_id_type=MESH,
            ).wait_recv()
            kind = jnp.where(j < 4, 1, 0)
            vecs = [rx[j, a] for a in range(8)]
            for n, (a, b) in enumerate(GRAM):
                prod = vecs[a] * vecs[b]
                part = (prod[:, 0:128] + prod[:, 128:256]) + (prod[:, 256:384] + prod[:, 384:512])
                gacc[kind, n] = gacc[kind, n] + part

    conv_taps(0, 0, 9)
    finish_forward(0)
    for j in range(4):
        cot_copy(j).wait()
    for j in range(4):
        we_copy(j).wait()
    pl.semaphore_wait(barrier, 22)

    def image_rows(g, carry):
        b, r = g // 4, g % 4
        rows = pl.ds(pl.multiple_of(g * 64, 64), 64)
        for h in range(2):
            spread(hg[h, rows], hs, b, r, slice(h * 256, h * 256 + 256))
        return carry

    def input_taps(first, last):
        def one(t, carry):
            wide = tap(hs, t)
            part = nt(wide[:, 0:256], wt[0, 8 - t]) + nt(wide[:, 256:512], wt[1, 8 - t])

            @pl.when(t == 0)
            def _():
                acc2[...] = part

            @pl.when(t > 0)
            def _():
                acc2[...] += part

            return carry

        lax.fori_loop(first, last, one, 0)

    def finish_input():
        kept = jnp.where(xin[...].reshape(1024, 512).astype(F32) > 0, acc2[...], 0.0)
        xin[...] = kept.astype(BF16).reshape(4, 16, 16, 512)
        pltpu.make_async_copy(xin, ig_hbm, out_sem).start()

    def iteration(p, carry):
        for k in range(2):

            @pl.when(p < PAIRS)
            def _():
                produce(p, k)
                step1(p, k)

        for lag, step in ((LAG2, step2), (LAG3, step3), (LAG4, step4), (LAG5, step5), (LAG6, step6)):

            @pl.when(jnp.logical_and(p >= lag, p < PAIRS + lag))
            def _():
                for k in range(2):
                    step(p - lag, k)

        @pl.when(jnp.logical_or(p < 2, jnp.logical_or(p == 6, p == 7)))
        def _():
            h = p // 6
            k0 = (p % 2) * 2
            hidden_back(h, k0, k0 + 2)

            @pl.when(p % 2 == 1)
            def _():
                finish_back(h)

        @pl.when(jnp.logical_and(p >= 2, p < 6))
        def _():
            conv_taps(1, ((p - 2) * 9) // 4, ((p - 1) * 9) // 4)

            @pl.when(p == 5)
            def _():
                finish_forward(1)

        @pl.when(p == 8)
        def _():
            lax.fori_loop(0, 16, image_rows, 0)

        @pl.when(jnp.logical_and(p >= 8, p < 13))
        def _():
            input_taps(((p - 8) * 9) // 5, ((p - 7) * 9) // 5)

            @pl.when(p == 12)
            def _():
                finish_input()

        return carry

    lax.fori_loop(0, PAIRS + LAG6, iteration, 0)

    lane = lax.broadcasted_iota(jnp.int32, (1, 128), 1)
    rows = []
    for kind in range(2):
        packed = jnp.zeros((1, 128), F32)
        for n in range(len(GRAM)):
            line = jnp.sum(gacc[kind, n], axis=0, keepdims=True)
            packed = jnp.where(lane == n, jnp.sum(line, axis=1, keepdims=True), packed)
        rows.append(packed)
    sub = lax.broadcasted_iota(jnp.int32, (8, 128), 0)
    mine = jnp.where(sub == 0, rows[0], jnp.where(sub == 1, rows[1], 0.0))

    def exchange(axis, me, count, value, src, dst, send, recv):
        src[...] = value
        dst[me] = value

        def go(d, carry):
            pltpu.make_async_remote_copy(
                src_ref=src, dst_ref=dst.at[me], send_sem=send, recv_sem=recv,
                device_id={axis: (me + d) % count}, device_id_type=MESH,
            ).start()
            return carry

        lax.fori_loop(1, count, go, 0)
        got = dst.at[pl.ds(0, count - 1)]
        pltpu.make_async_remote_copy(
            src_ref=got, dst_ref=got, send_sem=send, recv_sem=recv,
            device_id={axis: (me + 1) % count}, device_id_type=MESH,
        ).wait_recv()
        total = dst[0]
        for n in range(1, count):
            total = total + dst[n]
        return total

    total = exchange("outer", o, 8, mine, stat.at[0], st1, ss1, qs1)
    total = exchange("inner", i, 16, total, stat.at[1], st2, ss2, qs2)
    gram = {ab: jnp.broadcast_to(total[:, n : n + 1], (8, 128)) for ab, n in GRAM_AT.items()}
    weights = adasum_weights(gram)

    for kind, count, out in ((0, 9, fin_conv), (1, 4, fin_exp)):
        coef = [jnp.broadcast_to(jnp.tile(w[kind : kind + 1], (1, 4)), (4, 512)) for w in weights]
        for t in range(count):
            j = t if kind == 1 else t + 4
            value = coef[0] * rx[j, 0]
            for a in range(1, 8):
                value = value + coef[a] * rx[j, a]
            out[:, t * 512 : (t + 1) * 512] = value

    def drain(ref, send):
        pltpu.make_async_remote_copy(
            src_ref=ref, dst_ref=ref, send_sem=send, recv_sem=qs1,
            device_id={"outer": (o + 1) % 8}, device_id_type=MESH,
        ).wait_send()

    for ref, send in (
        (r1p, s1p), (r1m, s1m), (r2p, s2p), (r2m, s2m), (r3p, s3p), (r3m, s3m), (r4p, s4p), (r4m, s4m),
        (rx.at[:, pl.ds(0, 7)], sx), (st1.at[pl.ds(0, 7)], ss1), (st2.at[pl.ds(0, 15)], ss2),
    ):
        drain(ref, send)
    pltpu.make_async_copy(xin, ig_hbm, out_sem).wait()


def body(inputs, cotangent, conv_weight, expand_weight, conv_momentum, expand_momentum):
    images, height, across, channels = inputs.shape
    rows = images * height * across
    dma = pltpu.SemaphoreType.DMA
    vmem = pltpu.VMEM
    any_spec = pl.BlockSpec(memory_space=pl.ANY)
    vmem_spec = pl.BlockSpec(memory_space=pltpu.VMEM)
    input_grad, fin_conv, fin_exp = pl.pallas_call(
        kernel,
        out_shape=(
            jax.ShapeDtypeStruct(inputs.shape, BF16),
            jax.ShapeDtypeStruct((4, 4608), F32),
            jax.ShapeDtypeStruct((4, 2048), F32),
        ),
        in_specs=[any_spec] * 4,
        out_specs=(any_spec, vmem_spec, vmem_spec),
        scratch_shapes=[
            vmem((4, 16, 16, 512), BF16),
            vmem((3, 4, 18, 16, 512), BF16),
            vmem((2, 9, 512, 256), BF16),
            vmem((4, 512, 512), BF16),
            vmem((4, 1024, 512), BF16),
            vmem((1024, 256), F32),
            vmem((2, 1024, 256), BF16),
            vmem((2, 2, 256, 1024), BF16),
            vmem((2, 1024, 256), BF16),
            vmem((3, 4, 18, 16, 512), BF16),
            vmem((1024, 512), F32),
            vmem((256, 256), BF16),
            vmem((26, 4, 4, 16, 512), BF16),
            vmem((PAIRS, 2, 4, 16, 256), BF16),
            vmem((PAIRS, 2, 4, 16, 256), BF16),
            vmem((PAIRS, 2, 4, 16, 512), BF16),
            vmem((PAIRS, 2, 4, 16, 512), BF16),
            vmem((PAIRS, 2, 4, 16, 512), BF16),
            vmem((PAIRS, 2, 16, 256), BF16),
            vmem((PAIRS, 2, 16, 256), BF16),
            vmem((PAIRS, 2, 16, 512), BF16),
            vmem((PAIRS, 2, 16, 512), BF16),
            vmem((PAIRS, 2, 4, 4, 512), F32),
            vmem((13, 8, 4, 512), F32),
            vmem((2, len(GRAM), 4, 128), F32),
            vmem((2, 8, 128), F32),
            vmem((8, 8, 128), F32),
            vmem((16, 8, 128), F32),
            dma, dma((2, 9)), dma((4,)), dma((4,)), dma,
        ]
        + [dma((PAIRS, 2))] * 8
        + [dma((13,)), dma, dma]
        + [dma] * 11,
        compiler_params=pltpu.CompilerParams(
            collective_id=0, has_side_effects=True, vmem_limit_bytes=62 * 1024 * 1024
        ),
    )(inputs, cotangent.reshape(rows, cotangent.shape[-1]), conv_weight, expand_weight)
    conv_new = MOMENTUM * conv_momentum + fin_conv.reshape(conv_momentum.shape)
    expand_new = MOMENTUM * expand_momentum + fin_exp.reshape(expand_momentum.shape)
    return (input_grad, conv_new, expand_new)


def solution(mesh):
    return jax.shard_map(
        body,
        mesh=mesh,
        in_specs=(
            P(("outer", "inner"), None, None, None),
            P(("outer", "inner"), None, None, None),
            P(),
            P(),
            P(("outer", "inner"), None),
            P(("outer", "inner"), None),
        ),
        out_specs=(
            P(("outer", "inner"), None, None, None),
            P(("outer", "inner"), None),
            P(("outer", "inner"), None),
        ),
        check_vma=False,
    )
```

time: 256 us -> 93.6 us (0.37); the launches traced: 251 us -> 93.4 us
  Pallas kernels: 0 us -> 87.3 us
  waiting for transfers between devices: 85.3 us -> 0 us
  local copies, waits for them, and re-layouts: 66.8 us -> 4.02 us
  between operations: 29.9 us -> 0.68 us
  matrix products: 28 us -> 0 us
  starting transfers between devices: 20.9 us -> 0 us
  other arithmetic: 20 us -> 1.4 us
    pallas_call x0 -> x1, Pallas kernels: none -> 87.3 us  [body(): pl.pallas_call(kernel, out_shape=(jax.ShapeDtypeStruct(inputs.shape, BF16...]
    unnamed x2 -> x0, waiting for transfers between devices: 71.7 us -> none
    dot_general x5 -> x0, matrix products: 28 us -> none  [the longest x1 10 us: local_step(): input_back = jnp.dot(back_cols, flipped, preferred_element_type=jnp.float32)]
    reshape x4 -> x0, local copies, waits for them, and re-layouts: 20 us -> none  [the longest x2 15.5 us: body(): conv_grad.astype(jnp.float32).reshape(outer_count, inner_count, conv_len)]
    all_to_all x3 -> x0, starting transfers between devices: 14.7 us -> none  [sent_to_all(): lax.all_to_all(jnp.broadcast_to(x[None], (length, *x.shape)), axis, 0, 0,...]
    another operation x3 -> x0, local copies, waits for them, and re-layouts: 11.9 us -> none  [layer_stats(): jnp.stack([jnp.sum(conv_first * conv_first), jnp.sum(conv_second * conv_s...]
    all_to_all x3 -> x0, waiting for transfers between devices: 10.3 us -> none  [sent_to_all(): lax.all_to_all(jnp.broadcast_to(x[None], (length, *x.shape)), axis, 0, 0,...]
    unnamed x49 -> x7, local copies, waits for them, and re-layouts: 13.9 us -> 4.02 us
  transfers between devices with their start and end apart: 7 -> 0, of which waited for: 5 -> 0; matrix products, arithmetic and copies ran while one was open for 14% -> 0% of each run, Pallas kernels for 0% -> 0%
where the time goes in v1:
time: 93.6 us; the launch traced here: 93.4 us
  Pallas kernels  87.3 us (93%)
  local copies, waits for them, and re-layouts  4.02 us (4%)
  other arithmetic  1.4 us (1%)
    pallas_call x1, Pallas kernels, body(): pl.pallas_call(kernel, out_shape=(jax.ShapeDtypeStruct(inputs.shape, BF16...  87.3 us
    unnamed x7, local copies, waits for them, and re-layouts  4.02 us

profile of v1, /device:TPU:1, one launch (start us, length us, event | category | flops | bytes accessed | tf_op | source)
XLA Modules:
  0.0 93.4 jit_solution(2880764154610079151)
XLA Ops:
  0.6 0.0 copy-start
  0.6 0.0 copy-start.1
  0.7 87.3 %shard_map.85 = (bf16[4,16,16,512]{3,2,1,0:T(8,128)(2,1)}, f32[4,4608]{1,0:T(4,128)}, f32[4,2048]{1,0:T(4,128)}) custom-call(bf16[4,16,16,512]{3,2,1,0:T(8,128)(2,1)} %x_hbm.1, bf16[1024,2048]{1,0:T(8,128)(2,1)} %bitcast.7, bf16[4608,512]{1,0:T(8,128)(2,1)} %w_hbm.1, bf16[512,2048]{1,0:T(8,128)(2,1)} %we_hbm.1), custom_call_target="tpu_custom_call" | custom-call | tf_op jit(solution)/shard_map/pallas_call | solution.py:491
  87.9 1.0 %copy.9 = f32[1,1,4,4608]{3,1,2,0:T(1,128)S(1)} copy(f32[1,1,4,4608]{3,2,1,0:T(4,128)} %bitcast.10) | data formatting | bytes 147456
  88.9 0.0 copy-done
  88.9 0.7 multiply_add_fusion
  89.6 0.8 copy.10
  90.4 0.0 copy-done.1
  90.4 0.7 multiply_add_fusion.1
  91.1 2.3 %copy.12 = bf16[4,16,16,512]{3,2,1,0:T(8,128)(2,1)} copy(bf16[4,16,16,512]{3,2,1,0:T(8,128)(2,1)} %get-tuple-element.12) | data formatting | bytes 2097152
Async XLA Ops:
  0.6 88.3 %copy-start = (f32[1,18432]{1,0:T(1,128)S(1)}, f32[1,18432]{1,0:T(1,128)}, u32[]{:S(2)}) copy-start(f32[1,18432]{1,0:T(1,128)} %param.10) | copy-start | bytes 221188
  0.6 89.8 %copy-start.1 = (f32[1,8192]{1,0:T(1,128)S(1)}, f32[1,8192]{1,0:T(1,128)}, u32[]{:S(2)}) copy-start(f32[1,8192]{1,0:T(1,128)} %param.11) | copy-start | bytes 98308

commit v2 on v1

--- a/solution.py
+++ b/solution.py
@@ -12,7 +12,8 @@
 MESH = pl.DeviceIdType.MESH
 
 PAIRS = 13
-LAG2, LAG3, LAG4, LAG5, LAG6 = 1, 3, 4, 5, 7
+LAG2, LAG3, LAG4, LAG5, LAG6 = 2, 4, 6, 8, 10
+INPUT_AT = 9
 GRAM = [(a, b) for a in range(8) for b in range(a, 8)]
 GRAM_AT = {ab: n for n, ab in enumerate(GRAM)}
 
@@ -63,9 +64,9 @@
 def kernel(
     x_hbm, cot_hbm, w_hbm, we_hbm,
     ig_hbm, fin_conv, fin_exp,
-    xin, xs, wt, we, cot, acc, hp, ht, hg, hs, acc2, perm,
+    xin, xs, wt, wn, we, cot, acc, hp, ht, hg, hs, acc2, perm,
     gm, r1p, r1m, r2p, r2m, tb, r3p, r3m, r4p, r4m, ub, rx, gacc, stat, st1, st2,
-    in_sem, w_sem, we_sem, cot_sem, out_sem,
+    in_sem, w_sem, wn_sem, we_sem, cot_sem, out_sem,
     q1p, q1m, q2p, q2m, q3p, q3m, q4p, q4m, qx, qs1, qs2,
     s1p, s1m, s2p, s2m, s3p, s3m, s4p, s4m, sx, ss1, ss2,
 ):
@@ -87,104 +88,88 @@
     lax.fori_loop(1, 8, greet_outer, 0)
     lax.fori_loop(1, 16, greet_inner, 0)
 
-    def w_copy(h, t):
+    def w_copy(h, dy):
         return pltpu.make_async_copy(
-            w_hbm.at[pl.ds(pl.multiple_of(t * 512, 512), 512), pl.ds(pl.multiple_of(h * 256, 256), 256)],
-            wt.at[h, t],
-            w_sem.at[h, t],
-        )
-
-    def cot_copy(j):
-        return pltpu.make_async_copy(cot_hbm.at[:, pl.ds(j * 512, 512)], cot.at[j], cot_sem.at[j])
-
-    def we_copy(j):
-        return pltpu.make_async_copy(we_hbm.at[:, pl.ds(j * 512, 512)], we.at[j], we_sem.at[j])
-
+            w_hbm.at[pl.ds(dy * 1536, 1536), pl.ds(h * 256, 256)], wt.at[h, dy], w_sem.at[h, dy]
+        )
+
+    def wn_copies(ty):
+        return [
+            pltpu.make_async_copy(
+                w_hbm.at[pl.ds(((2 - ty) * 3 + 2 - tx) * 512, 512)],
+                wn.at[ty, :, pl.ds(tx * 512, 512)],
+                wn_sem.at[ty, tx],
+            )
+            for tx in range(3)
+        ]
+
+    cot_copy = pltpu.make_async_copy(cot_hbm, cot, cot_sem)
+    we_copy = pltpu.make_async_copy(we_hbm, we, we_sem)
     in_copy = pltpu.make_async_copy(x_hbm, xin, in_sem)
     in_copy.start()
-
-    def start_w(h):
-        def one(t, carry):
-            w_copy(h, t).start()
-            return carry
-
-        lax.fori_loop(0, 9, one, 0)
-
-    start_w(0)
-    for j in range(4):
-        cot_copy(j).start()
-    for j in range(4):
-        we_copy(j).start()
-    start_w(1)
+    for dy in range(3):
+        w_copy(0, dy).start()
+    cot_copy.start()
+    we_copy.start()
+    for dy in range(3):
+        w_copy(1, dy).start()
+    for ty in range(3):
+        for c in wn_copies(ty):
+            c.start()
 
     row = lax.broadcasted_iota(jnp.int32, (256, 256), 0)
     col = lax.broadcasted_iota(jnp.int32, (256, 256), 1)
     want = ((row // 4) % 4) * 64 + (row // 16) * 4 + row % 4
     perm[...] = jnp.where(want == col, 1.0, 0.0).astype(BF16)
 
-    zero_row = jnp.zeros((16, 512), BF16)
+    zero_row = jnp.zeros((16, 1536), BF16)
     for dst in (xs, hs):
-        for dx in range(3):
-            for b in range(4):
-                dst[dx, b, 0] = zero_row
-                dst[dx, b, 17] = zero_row
+        for b in range(4):
+            dst[b, 0] = zero_row
+            dst[b, 17] = zero_row
     gacc[...] = jnp.zeros_like(gacc)
 
-    def spread(value, dst, b, r, lanes):
+    def spread(value, dst, b, r, first):
         n = value.shape[1]
         w = lax.broadcasted_iota(jnp.int32, (64, n), 0) % 16
         wide = value.astype(F32)
         left = jnp.where(w == 0, 0.0, pltpu.roll(wide, 1, 0)).astype(BF16)
         right = jnp.where(w == 15, 0.0, pltpu.roll(wide, 63, 0)).astype(BF16)
         for dx, v in ((0, left), (1, value), (2, right)):
-            dst[dx, b, pl.ds(1 + 4 * r, 4), :, lanes] = v.reshape(4, 16, n)
+            at = dx * 512 + first
+            dst[b, pl.ds(1 + 4 * r, 4), :, at : at + n] = v.reshape(4, 16, n)
 
     in_copy.wait()
 
     def prep(g, carry):
         b, r = g // 4, g % 4
         v = xin[b, pl.ds(4 * r, 4)].reshape(64, 512)
-        spread(jnp.maximum(v, jnp.zeros((), BF16)), xs, b, r, slice(None))
+        spread(jnp.maximum(v, jnp.zeros((), BF16)), xs, b, r, 0)
         return carry
 
     lax.fori_loop(0, 16, prep, 0)
 
-    def tap(ref, t):
-        return ref[t % 3, :, pl.ds(t // 3, 16)].reshape(1024, 512)
-
-    def conv_taps(h, first, last):
-        def one(t, carry):
-            w_copy(h, t).wait()
-            part = nn(tap(xs, t), wt[h, t])
-
-            @pl.when(t == 0)
-            def _():
-                acc[...] = part
-
-            @pl.when(t > 0)
-            def _():
-                acc[...] += part
-
-            return carry
-
-        lax.fori_loop(first, last, one, 0)
+    def tap_row(ref, dy):
+        return ref[:, pl.ds(dy, 16)].reshape(1024, 1536)
+
+    def conv_taps(h, dy, first):
+        w_copy(h, dy).wait()
+        part = nn(tap_row(xs, dy), wt[h, dy])
+        if first:
+            acc[...] = part
+        else:
+            acc[...] += part
 
     def finish_forward(h):
         pre = acc[...].astype(BF16)
         hp[h] = pre
         ht[0, h] = nt(perm[...], jnp.maximum(pre, jnp.zeros((), BF16))).astype(BF16)
 
-    def hidden_back(h, first, last):
-        def one(k, carry):
-            rows = pl.ds(pl.multiple_of(k * 256, 256), 256)
-            chans = pl.ds(pl.multiple_of(h * 256, 256), 256)
-            back = nt(cot[0, rows], we[0, chans])
-            for j in range(1, 4):
-                back = back + nt(cot[j, rows], we[j, chans])
-            hg[h, rows] = jnp.where(hp[h, rows].astype(F32) > 0, back, 0.0).astype(BF16)
-            return carry
-
-        lax.fori_loop(first, last, one, 0)
+    def hidden_back(h, k):
+        rows = pl.ds(pl.multiple_of(k * 512, 512), 512)
+        chans = pl.ds(pl.multiple_of(h * 256, 256), 256)
+        back = nt(cot[rows], we[chans])
+        hg[h, rows] = jnp.where(hp[h, rows].astype(F32) > 0, back, 0.0).astype(BF16)
 
     def finish_back(h):
         ht[1, h] = nt(perm[...], hg[h]).astype(BF16)
@@ -196,12 +181,14 @@
 
         @pl.when(j < 4)
         def _():
-            g = nn(ht[0, h], cot[j]) * (1.0 / 1024.0)
+            g = nn(ht[0, h], cot[:, pl.ds(pl.multiple_of(j * 512, 512), 512)]) * (1.0 / 1024.0)
             gm[q] = g.astype(BF16).reshape(4, 4, 16, 512)
 
         @pl.when(j >= 4)
         def _():
-            g = nn(ht[1, h], tap(xs, j - 4)) * (1.0 / 1024.0)
+            t = j - 4
+            at = pl.multiple_of((t % 3) * 512, 512)
+            g = nn(ht[1, h], xs[:, pl.ds(t // 3, 16), :, pl.ds(at, 512)].reshape(1024, 512)) * (1.0 / 1024.0)
             gm[q] = g.astype(BF16).reshape(4, 4, 16, 512)
 
     def ring(k, stage):
@@ -334,42 +321,54 @@
                 part = (prod[:, 0:128] + prod[:, 128:256]) + (prod[:, 256:384] + prod[:, 384:512])
                 gacc[kind, n] = gacc[kind, n] + part
 
-    conv_taps(0, 0, 9)
+    for dy in range(3):
+        conv_taps(0, dy, dy == 0)
     finish_forward(0)
-    for j in range(4):
-        cot_copy(j).wait()
-    for j in range(4):
-        we_copy(j).wait()
+    cot_copy.wait()
+    we_copy.wait()
     pl.semaphore_wait(barrier, 22)
 
     def image_rows(g, carry):
         b, r = g // 4, g % 4
         rows = pl.ds(pl.multiple_of(g * 64, 64), 64)
         for h in range(2):
-            spread(hg[h, rows], hs, b, r, slice(h * 256, h * 256 + 256))
+            spread(hg[h, rows], hs, b, r, h * 256)
         return carry
 
-    def input_taps(first, last):
-        def one(t, carry):
-            wide = tap(hs, t)
-            part = nt(wide[:, 0:256], wt[0, 8 - t]) + nt(wide[:, 256:512], wt[1, 8 - t])
-
-            @pl.when(t == 0)
-            def _():
-                acc2[...] = part
-
-            @pl.when(t > 0)
-            def _():
-                acc2[...] += part
-
-            return carry
-
-        lax.fori_loop(first, last, one, 0)
-
-    def finish_input():
-        kept = jnp.where(xin[...].reshape(1024, 512).astype(F32) > 0, acc2[...], 0.0)
-        xin[...] = kept.astype(BF16).reshape(4, 16, 16, 512)
-        pltpu.make_async_copy(xin, ig_hbm, out_sem).start()
+    def input_piece(ty, m):
+        part = nt(hs[pl.ds(2 * m, 2), pl.ds(ty, 16)].reshape(512, 1536), wn[ty])
+        rows = pl.ds(pl.multiple_of(512 * m, 512), 512)
+        if ty == 0:
+            acc2[rows] = part
+        elif ty == 1:
+            acc2[rows] += part
+        else:
+            images = pl.ds(2 * m, 2)
+            total = acc2[rows] + part
+            kept = jnp.where(xin[images].reshape(512, 512).astype(F32) > 0, total, 0.0)
+            xin[images] = kept.astype(BF16).reshape(2, 16, 16, 512)
+
+    def input_work(p):
+        @pl.when(p == INPUT_AT - 1)
+        def _():
+            lax.fori_loop(0, 16, image_rows, 0)
+
+        for ty in range(3):
+
+            @pl.when(jnp.logical_and(p >= INPUT_AT + 2 * ty, p < INPUT_AT + 2 * ty + 2))
+            def _():
+                m = p - (INPUT_AT + 2 * ty)
+
+                @pl.when(m == 0)
+                def _():
+                    for c in wn_copies(ty):
+                        c.wait()
+
+                input_piece(ty, m)
+
+        @pl.when(p == INPUT_AT + 5)
+        def _():
+            pltpu.make_async_copy(xin, ig_hbm, out_sem).start()
 
     def iteration(p, carry):
         for k in range(2):
@@ -389,33 +388,25 @@
         @pl.when(jnp.logical_or(p < 2, jnp.logical_or(p == 6, p == 7)))
         def _():
             h = p // 6
-            k0 = (p % 2) * 2
-            hidden_back(h, k0, k0 + 2)
+            hidden_back(h, p % 2)
 
             @pl.when(p % 2 == 1)
             def _():
                 finish_back(h)
 
-        @pl.when(jnp.logical_and(p >= 2, p < 6))
-        def _():
-            conv_taps(1, ((p - 2) * 9) // 4, ((p - 1) * 9) // 4)
-
-            @pl.when(p == 5)
+        @pl.when(p == 2)
+        def _():
+            conv_taps(1, 0, True)
+
+        @pl.when(jnp.logical_or(p == 3, p == 4))
+        def _():
+            conv_taps(1, p - 2, False)
+
+            @pl.when(p == 4)
             def _():
                 finish_forward(1)
 
-        @pl.when(p == 8)
-        def _():
-            lax.fori_loop(0, 16, image_rows, 0)
-
-        @pl.when(jnp.logical_and(p >= 8, p < 13))
-        def _():
-            input_taps(((p - 8) * 9) // 5, ((p - 7) * 9) // 5)
-
-            @pl.when(p == 12)
-            def _():
-                finish_input()
-
+        input_work(p)
         return carry
 
     lax.fori_loop(0, PAIRS + LAG6, iteration, 0)
@@ -479,6 +470,26 @@
     ):
         drain(ref, send)
     pltpu.make_async_copy(xin, ig_hbm, out_sem).wait()
+
+
+def update_kernel(ig, fin_conv, fin_exp, mom_conv, mom_exp, ig_out, new_conv, new_exp, buf, in_sem, out_sem):
+    def fetch(b):
+        return pltpu.make_async_copy(ig.at[b], buf.at[b], in_sem.at[b])
+
+    def put(b):
+        return pltpu.make_async_copy(buf.at[b], ig_out.at[b], out_sem.at[b])
+
+    for b in range(4):
+        fetch(b).start()
+    for fin, mom, new in ((fin_conv, mom_conv, new_conv), (fin_exp, mom_exp, new_exp)):
+        n = fin.shape[1]
+        for s in range(4):
+            new[0:1, s * n : (s + 1) * n] = MOMENTUM * mom[0:1, s * n : (s + 1) * n] + fin[s : s + 1, :]
+    for b in range(4):
+        fetch(b).wait()
+        put(b).start()
+    for b in range(4):
+        put(b).wait()
 
 
 def body(inputs, cotangent, conv_weight, expand_weight, conv_momentum, expand_momentum):
@@ -499,15 +510,16 @@
         out_specs=(any_spec, vmem_spec, vmem_spec),
         scratch_shapes=[
             vmem((4, 16, 16, 512), BF16),
-            vmem((3, 4, 18, 16, 512), BF16),
-            vmem((2, 9, 512, 256), BF16),
-            vmem((4, 512, 512), BF16),
-            vmem((4, 1024, 512), BF16),
+            vmem((4, 18, 16, 1536), BF16),
+            vmem((2, 3, 1536, 256), BF16),
+            vmem((3, 512, 1536), BF16),
+            vmem((512, 2048), BF16),
+            vmem((1024, 2048), BF16),
             vmem((1024, 256), F32),
             vmem((2, 1024, 256), BF16),
             vmem((2, 2, 256, 1024), BF16),
             vmem((2, 1024, 256), BF16),
-            vmem((3, 4, 18, 16, 512), BF16),
+            vmem((4, 18, 16, 1536), BF16),
             vmem((1024, 512), F32),
             vmem((256, 256), BF16),
             vmem((26, 4, 4, 16, 512), BF16),
@@ -526,7 +538,7 @@
             vmem((2, 8, 128), F32),
             vmem((8, 8, 128), F32),
             vmem((16, 8, 128), F32),
-            dma, dma((2, 9)), dma((4,)), dma((4,)), dma,
+            dma, dma((2, 3)), dma((3, 3)), dma, dma, dma,
         ]
         + [dma((PAIRS, 2))] * 8
         + [dma((13,)), dma, dma]
@@ -535,9 +547,17 @@
             collective_id=0, has_side_effects=True, vmem_limit_bytes=62 * 1024 * 1024
         ),
     )(inputs, cotangent.reshape(rows, cotangent.shape[-1]), conv_weight, expand_weight)
-    conv_new = MOMENTUM * conv_momentum + fin_conv.reshape(conv_momentum.shape)
-    expand_new = MOMENTUM * expand_momentum + fin_exp.reshape(expand_momentum.shape)
-    return (input_grad, conv_new, expand_new)
+    return pl.pallas_call(
+        update_kernel,
+        out_shape=(
+            jax.ShapeDtypeStruct(inputs.shape, BF16),
+            jax.ShapeDtypeStruct(conv_momentum.shape, F32),
+            jax.ShapeDtypeStruct(expand_momentum.shape, F32),
+        ),
+        in_specs=[any_spec] + [vmem_spec] * 4,
+        out_specs=(any_spec, vmem_spec, vmem_spec),
+        scratch_shapes=[vmem((4, 16, 16, 512), BF16), dma((4,)), dma((4,))],
+    )(input_grad, fin_conv, fin_exp, conv_momentum, expand_momentum)
 
 
 def solution(mesh):

time: 93.6 us -> 78.5 us (0.84)
  Pallas kernels: 87.3 us -> 77.7 us
  local copies, waits for them, and re-layouts: 4.02 us -> 0 us
  other arithmetic: 1.4 us -> 0 us
    pallas_call x1, Pallas kernels: 87.3 us -> 74.1 us  [body(): pl.pallas_call(kernel, out_shape=(jax.ShapeDtypeStruct(inputs.shape, BF16...]
    unnamed x7 -> x0, local copies, waits for them, and re-layouts: 4.02 us -> none
    pallas_call x0 -> x1, Pallas kernels: none -> 3.56 us  [body(): pl.pallas_call(update_kernel, out_shape=(jax.ShapeDtypeStruct(inputs.shap...]
    add x2 -> x0, other arithmetic: 1.4 us -> none  [the longest x1 0.74 us: body(): conv_new = MOMENTUM * conv_momentum + fin_conv.reshape(conv_momentum.shape)]
where the time goes in v2:
time: 78.5 us; the launch traced here: 78.3 us
  Pallas kernels  77.7 us (99%)
    pallas_call x1, Pallas kernels, body(): pl.pallas_call(kernel, out_shape=(jax.ShapeDtypeStruct(inputs.shape, BF16...  74.1 us
    pallas_call x1, Pallas kernels, body(): pl.pallas_call(update_kernel, out_shape=(jax.ShapeDtypeStruct(inputs.shap...  3.56 us

profile of v2, /device:TPU:1, one launch (start us, length us, event | category | flops | bytes accessed | tf_op | source)
XLA Modules:
  0.0 78.3 jit_solution(2847650586589681088)
XLA Ops:
  0.6 74.1 %shard_map.85 = (bf16[4,16,16,512]{3,2,1,0:T(8,128)(2,1)}, f32[4,4608]{1,0:T(4,128)}, f32[4,2048]{1,0:T(4,128)}) custom-call(bf16[4,16,16,512]{3,2,1,0:T(8,128)(2,1)} %x_hbm.1, bf16[1024,2048]{1,0:T(8,128)(2,1)} %bitcast.1, bf16[4608,512]{1,0:T(8,128)(2,1)} %w_hbm.1, bf16[512,2048]{1,0:T(8,128)(2,1)} %we_hbm.1), custom_call_target="tpu_custom_call" | custom-call | tf_op jit(solution)/shard_map/pallas_call | solution.py:502
  74.7 3.6 %shard_map.86 = (bf16[4,16,16,512]{3,2,1,0:T(8,128)(2,1)}, f32[1,18432]{1,0:T(1,128)}, f32[1,8192]{1,0:T(1,128)}) custom-call(bf16[4,16,16,512]{3,2,1,0:T(8,128)(2,1)} %get-tuple-element.6.ig, f32[4,4608]{1,0:T(4,128)} %get-tuple-element.7.fin_conv, f32[4,2048]{1,0:T(4,128)} %get-tuple-element.8.fin_exp, f32[1,18432]{1,0:T(1,128)} %mom_conv.1, f32[1,8192]{1,0:T(1,128)} %mom_exp.1), custom_call_target="tpu_custom_call" | custom-call | tf_op jit(solution)/shard_map/pallas_call | solution.py:550

commit v3 on v2

--- a/solution.py
+++ b/solution.py
@@ -14,6 +14,7 @@
 PAIRS = 13
 LAG2, LAG3, LAG4, LAG5, LAG6 = 2, 4, 6, 8, 10
 INPUT_AT = 9
+VMEM_LIMIT = 56 * 1024 * 1024
 GRAM = [(a, b) for a in range(8) for b in range(a, 8)]
 GRAM_AT = {ab: n for n, ab in enumerate(GRAM)}
 
@@ -63,10 +64,10 @@
 
 def kernel(
     x_hbm, cot_hbm, w_hbm, we_hbm,
-    ig_hbm, fin_conv, fin_exp,
+    ig, fin_conv, fin_exp,
     xin, xs, wt, wn, we, cot, acc, hp, ht, hg, hs, acc2, perm,
     gm, r1p, r1m, r2p, r2m, tb, r3p, r3m, r4p, r4m, ub, rx, gacc, stat, st1, st2,
-    in_sem, w_sem, wn_sem, we_sem, cot_sem, out_sem,
+    in_sem, w_sem, wn_sem, we_sem, cot_sem,
     q1p, q1m, q2p, q2m, q3p, q3m, q4p, q4m, qx, qs1, qs2,
     s1p, s1m, s2p, s2m, s3p, s3m, s4p, s4m, sx, ss1, ss2,
 ):
@@ -105,8 +106,9 @@
 
     cot_copy = pltpu.make_async_copy(cot_hbm, cot, cot_sem)
     we_copy = pltpu.make_async_copy(we_hbm, we, we_sem)
-    in_copy = pltpu.make_async_copy(x_hbm, xin, in_sem)
-    in_copy.start()
+    in_copies = [pltpu.make_async_copy(x_hbm.at[b], xin.at[b], in_sem.at[b]) for b in range(4)]
+    for c in in_copies:
+        c.start()
     for dy in range(3):
         w_copy(0, dy).start()
     cot_copy.start()
@@ -139,15 +141,16 @@
             at = dx * 512 + first
             dst[b, pl.ds(1 + 4 * r, 4), :, at : at + n] = v.reshape(4, 16, n)
 
-    in_copy.wait()
-
-    def prep(g, carry):
-        b, r = g // 4, g % 4
-        v = xin[b, pl.ds(4 * r, 4)].reshape(64, 512)
-        spread(jnp.maximum(v, jnp.zeros((), BF16)), xs, b, r, 0)
-        return carry
-
-    lax.fori_loop(0, 16, prep, 0)
+
+    for b in range(4):
+        in_copies[b].wait()
+
+        def prep(r, carry, b=b):
+            v = xin[b, pl.ds(4 * r, 4)].reshape(64, 512)
+            spread(jnp.maximum(v, jnp.zeros((), BF16)), xs, b, r, 0)
+            return carry
+
+        lax.fori_loop(0, 4, prep, 0)
 
     def tap_row(ref, dy):
         return ref[:, pl.ds(dy, 16)].reshape(1024, 1536)
@@ -346,7 +349,7 @@
             images = pl.ds(2 * m, 2)
             total = acc2[rows] + part
             kept = jnp.where(xin[images].reshape(512, 512).astype(F32) > 0, total, 0.0)
-            xin[images] = kept.astype(BF16).reshape(2, 16, 16, 512)
+            ig[images] = kept.astype(BF16).reshape(2, 16, 16, 512)
 
     def input_work(p):
         @pl.when(p == INPUT_AT - 1)
@@ -365,10 +368,6 @@
                         c.wait()
 
                 input_piece(ty, m)
-
-        @pl.when(p == INPUT_AT + 5)
-        def _():
-            pltpu.make_async_copy(xin, ig_hbm, out_sem).start()
 
     def iteration(p, carry):
         for k in range(2):
@@ -469,27 +468,16 @@
         (rx.at[:, pl.ds(0, 7)], sx), (st1.at[pl.ds(0, 7)], ss1), (st2.at[pl.ds(0, 15)], ss2),
     ):
         drain(ref, send)
-    pltpu.make_async_copy(xin, ig_hbm, out_sem).wait()
-
-
-def update_kernel(ig, fin_conv, fin_exp, mom_conv, mom_exp, ig_out, new_conv, new_exp, buf, in_sem, out_sem):
-    def fetch(b):
-        return pltpu.make_async_copy(ig.at[b], buf.at[b], in_sem.at[b])
-
-    def put(b):
-        return pltpu.make_async_copy(buf.at[b], ig_out.at[b], out_sem.at[b])
-
-    for b in range(4):
-        fetch(b).start()
+
+
+def update_kernel(ig, fin_conv, fin_exp, mom_conv, mom_exp, ig_out, new_conv, new_exp, out_sem):
+    copy = pltpu.make_async_copy(ig, ig_out, out_sem)
+    copy.start()
     for fin, mom, new in ((fin_conv, mom_conv, new_conv), (fin_exp, mom_exp, new_exp)):
         n = fin.shape[1]
         for s in range(4):
             new[0:1, s * n : (s + 1) * n] = MOMENTUM * mom[0:1, s * n : (s + 1) * n] + fin[s : s + 1, :]
-    for b in range(4):
-        fetch(b).wait()
-        put(b).start()
-    for b in range(4):
-        put(b).wait()
+    copy.wait()
 
 
 def body(inputs, cotangent, conv_weight, expand_weight, conv_momentum, expand_momentum):
@@ -501,13 +489,9 @@
     vmem_spec = pl.BlockSpec(memory_space=pltpu.VMEM)
     input_grad, fin_conv, fin_exp = pl.pallas_call(
         kernel,
-        out_shape=(
-            jax.ShapeDtypeStruct(inputs.shape, BF16),
-            jax.ShapeDtypeStruct((4, 4608), F32),
-            jax.ShapeDtypeStruct((4, 2048), F32),
-        ),
+        out_shape=(vmem(inputs.shape, BF16), vmem((4, 4608), F32), vmem((4, 2048), F32)),
         in_specs=[any_spec] * 4,
-        out_specs=(any_spec, vmem_spec, vmem_spec),
+        out_specs=(vmem_spec, vmem_spec, vmem_spec),
         scratch_shapes=[
             vmem((4, 16, 16, 512), BF16),
             vmem((4, 18, 16, 1536), BF16),
@@ -538,13 +522,13 @@
             vmem((2, 8, 128), F32),
             vmem((8, 8, 128), F32),
             vmem((16, 8, 128), F32),
-            dma, dma((2, 3)), dma((3, 3)), dma, dma, dma,
+            dma((4,)), dma((2, 3)), dma((3, 3)), dma, dma,
         ]
         + [dma((PAIRS, 2))] * 8
         + [dma((13,)), dma, dma]
         + [dma] * 11,
         compiler_params=pltpu.CompilerParams(
-            collective_id=0, has_side_effects=True, vmem_limit_bytes=62 * 1024 * 1024
+            collective_id=0, has_side_effects=True, vmem_limit_bytes=VMEM_LIMIT
         ),
     )(inputs, cotangent.reshape(rows, cotangent.shape[-1]), conv_weight, expand_weight)
     return pl.pallas_call(
@@ -554,9 +538,10 @@
             jax.ShapeDtypeStruct(conv_momentum.shape, F32),
             jax.ShapeDtypeStruct(expand_momentum.shape, F32),
         ),
-        in_specs=[any_spec] + [vmem_spec] * 4,
+        in_specs=[vmem_spec] * 5,
         out_specs=(any_spec, vmem_spec, vmem_spec),
-        scratch_shapes=[vmem((4, 16, 16, 512), BF16), dma((4,)), dma((4,))],
+        scratch_shapes=[dma],
+        compiler_params=pltpu.CompilerParams(vmem_limit_bytes=8 * 1024 * 1024),
     )(input_grad, fin_conv, fin_exp, conv_momentum, expand_momentum)
 
 

time: 78.5 us -> 75.3 us (0.959)
  Pallas kernels: 77.7 us -> 74.5 us
    pallas_call x1, Pallas kernels: 3.56 us -> 1.62 us  [body(): pl.pallas_call(update_kernel, out_shape=(jax.ShapeDtypeStruct(inputs.shap...]
    pallas_call x1, Pallas kernels: 74.1 us -> 72.9 us  [body(): pl.pallas_call(kernel, out_shape=(vmem(inputs.shape, BF16), vmem((4, 4608...]
where the time goes in v3:
time: 75.3 us; the launch traced here: 75.2 us
  Pallas kernels  74.5 us (99%)
    pallas_call x1, Pallas kernels, body(): pl.pallas_call(kernel, out_shape=(vmem(inputs.shape, BF16), vmem((4, 4608...  72.9 us
    pallas_call x1, Pallas kernels, body(): pl.pallas_call(update_kernel, out_shape=(jax.ShapeDtypeStruct(inputs.shap...  1.62 us

profile of v3, /device:TPU:1, one launch (start us, length us, event | category | flops | bytes accessed | tf_op | source)
XLA Modules:
  0.0 75.2 jit_solution(16994112046405955733)
XLA Ops:
  0.6 0.0 copy-start
  0.6 0.0 copy-start.1
  0.7 72.9 %shard_map.85 = (bf16[4,16,16,512]{3,2,1,0:T(8,128)(2,1)S(1)}, f32[4,4608]{1,0:T(4,128)S(1)}, f32[4,2048]{1,0:T(4,128)S(1)}) custom-call(bf16[4,16,16,512]{3,2,1,0:T(8,128)(2,1)} %x_hbm.1, bf16[1024,2048]{1,0:T(8,128)(2,1)} %bitcast.1, bf16[4608,512]{1,0:T(8,128)(2,1)} %w_hbm.1, bf16[512,2048]{1,0:T(8,128)(2,1)} %we_hbm.1), custom_call_target="tpu_custom_call" | custom-call | tf_op jit(solution)/shard_map/pallas_call | solution.py:490
  73.5 0.0 copy-done
  73.5 0.0 copy-done.1
  73.5 1.6 %shard_map.86 = (bf16[4,16,16,512]{3,2,1,0:T(8,128)(2,1)}, f32[1,18432]{1,0:T(1,128)}, f32[1,8192]{1,0:T(1,128)}) custom-call(bf16[4,16,16,512]{3,2,1,0:T(8,128)(2,1)S(1)} %get-tuple-element.6.ig, f32[4,4608]{1,0:T(4,128)S(1)} %get-tuple-element.7.fin_conv, f32[4,2048]{1,0:T(4,128)S(1)} %get-tuple-element.8.fin_exp, f32[1,18432]{1,0:T(1,128)S(1)} %copy-done, ...), custom_call_target="tpu_custom_call" | custom-call | tf_op jit(solution)/shard_map/pallas_call | solution.py:534
Async XLA Ops:
  0.6 72.9 %copy-start = (f32[1,18432]{1,0:T(1,128)S(1)}, f32[1,18432]{1,0:T(1,128)}, u32[]{:S(2)}) copy-start(f32[1,18432]{1,0:T(1,128)} %mom_conv.1) | copy-start | bytes 221188
  0.6 72.9 %copy-start.1 = (f32[1,8192]{1,0:T(1,128)S(1)}, f32[1,8192]{1,0:T(1,128)}, u32[]{:S(2)}) copy-start(f32[1,8192]{1,0:T(1,128)} %mom_exp.1) | copy-start | bytes 98308

commit v4 on v3

--- a/solution.py
+++ b/solution.py
@@ -12,7 +12,7 @@
 MESH = pl.DeviceIdType.MESH
 
 PAIRS = 13
-LAG2, LAG3, LAG4, LAG5, LAG6 = 2, 4, 6, 8, 10
+LAG2, LAG3, LAG4, LAG5, LAG6 = 2, 4, 6, 8, 13
 INPUT_AT = 9
 VMEM_LIMIT = 56 * 1024 * 1024
 GRAM = [(a, b) for a in range(8) for b in range(a, 8)]
@@ -199,6 +199,9 @@
             return z, ((z + 1) % 4) * 4 + y, ((z + 3) % 4) * 4 + y
         return y, z * 4 + (y + 1) % 4, z * 4 + (y + 3) % 4
 
+    def opposite(k):
+        return z * 4 + (y + 2) % 4 if k == 0 else ((z + 2) % 4) * 4 + y
+
     def block(p, k, at):
         q = 2 * p + k
         return gm.at[q, at] if k == 0 else gm.at[q, :, at]
@@ -226,8 +229,10 @@
             remote(block(p, k, (at + 3) % 4), r2m.at[p, k], s2m, q2m.at[p, k], prv),
         )
 
-    def copies3(p, k):
+    def copies3(p, k, last=False):
         at, nxt, prv = ring(k, 1)
+        if last:
+            nxt = prv = opposite(k)
         far = tb.at[p, k, (at + 2) % 4]
         return (
             remote(far.at[:, LO], r3p.at[p, k], s3p, q3p.at[p, k], nxt),
@@ -265,21 +270,31 @@
         mine = block(p, k, at)
         total = mine[...].astype(F32) + r2p[p, k].astype(F32) + r2m[p, k].astype(F32)
         tb[p, k] = total.astype(BF16)
-        for c in copies3(p, k):
-            c.start()
+
+        @pl.when(p < PAIRS - 1)
+        def _():
+            for c in copies3(p, k):
+                c.start()
+
+        @pl.when(p == PAIRS - 1)
+        def _():
+            for c in copies3(p, k, last=True) + copies4(p, k):
+                c.start()
 
     def step4(p, k):
-        at, _, _ = ring(k, 1)
-        fwd, bwd = copies3(p, k)
-        out_fwd, out_bwd = copies4(p, k)
-        near = tb.at[p, k, (at + 1) % 4]
-        fwd.wait_recv()
-        near[:, LO] = (near[:, LO].astype(F32) + r3p[p, k].astype(F32)).astype(BF16)
-        out_fwd.start()
-        near = tb.at[p, k, (at + 3) % 4]
-        bwd.wait_recv()
-        near[:, HI] = (near[:, HI].astype(F32) + r3m[p, k].astype(F32)).astype(BF16)
-        out_bwd.start()
+        @pl.when(p < PAIRS - 1)
+        def _():
+            at, _, _ = ring(k, 1)
+            fwd, bwd = copies3(p, k)
+            out_fwd, out_bwd = copies4(p, k)
+            near = tb.at[p, k, (at + 1) % 4]
+            fwd.wait_recv()
+            near[:, LO] = (near[:, LO].astype(F32) + r3p[p, k].astype(F32)).astype(BF16)
+            out_fwd.start()
+            near = tb.at[p, k, (at + 3) % 4]
+            bwd.wait_recv()
+            near[:, HI] = (near[:, HI].astype(F32) + r3m[p, k].astype(F32)).astype(BF16)
+            out_bwd.start()
 
     def x_copy(p, k, part, j, dest):
         return pltpu.make_async_remote_copy(
@@ -294,7 +309,16 @@
         j = q % 13
         for c in copies4(p, k):
             c.wait_recv()
-        total = tb[p, k, at].astype(F32) + r4p[p, k].astype(F32) + r4m[p, k].astype(F32)
+        tail = tb.at[p, k, at]
+
+        @pl.when(p == PAIRS - 1)
+        def _():
+            for c in copies3(p, k, last=True):
+                c.wait_recv()
+            tail[:, LO] = (tail[:, LO].astype(F32) + r3p[p, k].astype(F32)).astype(BF16)
+            tail[:, HI] = (tail[:, HI].astype(F32) + r3m[p, k].astype(F32)).astype(BF16)
+
+        total = tail[...].astype(F32) + r4p[p, k].astype(F32) + r4m[p, k].astype(F32)
         for part in range(4):
             dest = h * 4 + part
             ub[p, k, part] = total[4 * part : 4 * part + 4]
@@ -418,8 +442,8 @@
             line = jnp.sum(gacc[kind, n], axis=0, keepdims=True)
             packed = jnp.where(lane == n, jnp.sum(line, axis=1, keepdims=True), packed)
         rows.append(packed)
-    sub = lax.broadcasted_iota(jnp.int32, (8, 128), 0)
-    mine = jnp.where(sub == 0, rows[0], jnp.where(sub == 1, rows[1], 0.0))
+    sub = lax.broadcasted_iota(jnp.int32, (2, 128), 0)
+    mine = jnp.where(sub == 0, rows[0], rows[1])
 
     def exchange(axis, me, count, value, src, dst, send, recv):
         src[...] = value
@@ -445,7 +469,7 @@
 
     total = exchange("outer", o, 8, mine, stat.at[0], st1, ss1, qs1)
     total = exchange("inner", i, 16, total, stat.at[1], st2, ss2, qs2)
-    gram = {ab: jnp.broadcast_to(total[:, n : n + 1], (8, 128)) for ab, n in GRAM_AT.items()}
+    gram = {ab: jnp.broadcast_to(total[:, n : n + 1], (2, 128)) for ab, n in GRAM_AT.items()}
     weights = adasum_weights(gram)
 
     for kind, count, out in ((0, 9, fin_conv), (1, 4, fin_exp)):
@@ -519,9 +543,9 @@
             vmem((PAIRS, 2, 4, 4, 512), F32),
             vmem((13, 8, 4, 512), F32),
             vmem((2, len(GRAM), 4, 128), F32),
-            vmem((2, 8, 128), F32),
-            vmem((8, 8, 128), F32),
-            vmem((16, 8, 128), F32),
+            vmem((2, 2, 128), F32),
+            vmem((8, 2, 128), F32),
+            vmem((16, 2, 128), F32),
             dma((4,)), dma((2, 3)), dma((3, 3)), dma, dma,
         ]
         + [dma((PAIRS, 2))] * 8

time: 75.3 us -> 74.3 us (0.987)
  Pallas kernels: 74.5 us -> 73.5 us
    pallas_call x1, Pallas kernels: 72.9 us -> 71.9 us  [body(): pl.pallas_call(kernel, out_shape=(vmem(inputs.shape, BF16), vmem((4, 4608...]
where the time goes in v4:
time: 74.3 us; the launch traced here: 74.2 us
  Pallas kernels  73.5 us (99%)
    pallas_call x1, Pallas kernels, body(): pl.pallas_call(kernel, out_shape=(vmem(inputs.shape, BF16), vmem((4, 4608...  71.9 us
    pallas_call x1, Pallas kernels, body(): pl.pallas_call(update_kernel, out_shape=(jax.ShapeDtypeStruct(inputs.shap...  1.62 us

profile of v4, /device:TPU:1, one launch (start us, length us, event | category | flops | bytes accessed | tf_op | source)
XLA Modules:
  0.0 74.2 jit_solution(7889006263515211680)
XLA Ops:
  0.6 0.0 copy-start
  0.6 0.0 copy-start.1
  0.7 71.9 %shard_map.85 = (bf16[4,16,16,512]{3,2,1,0:T(8,128)(2,1)S(1)}, f32[4,4608]{1,0:T(4,128)S(1)}, f32[4,2048]{1,0:T(4,128)S(1)}) custom-call(bf16[4,16,16,512]{3,2,1,0:T(8,128)(2,1)} %x_hbm.1, bf16[1024,2048]{1,0:T(8,128)(2,1)} %bitcast.1, bf16[4608,512]{1,0:T(8,128)(2,1)} %w_hbm.1, bf16[512,2048]{1,0:T(8,128)(2,1)} %we_hbm.1), custom_call_target="tpu_custom_call" | custom-call | tf_op jit(solution)/shard_map/pallas_call | solution.py:514
  72.6 0.0 copy-done
  72.6 0.0 copy-done.1
  72.6 1.6 %shard_map.86 = (bf16[4,16,16,512]{3,2,1,0:T(8,128)(2,1)}, f32[1,18432]{1,0:T(1,128)}, f32[1,8192]{1,0:T(1,128)}) custom-call(bf16[4,16,16,512]{3,2,1,0:T(8,128)(2,1)S(1)} %get-tuple-element.6.ig, f32[4,4608]{1,0:T(4,128)S(1)} %get-tuple-element.7.fin_conv, f32[4,2048]{1,0:T(4,128)S(1)} %get-tuple-element.8.fin_exp, f32[1,18432]{1,0:T(1,128)S(1)} %copy-done, ...), custom_call_target="tpu_custom_call" | custom-call | tf_op jit(solution)/shard_map/pallas_call | solution.py:558
Async XLA Ops:
  0.6 71.9 %copy-start = (f32[1,18432]{1,0:T(1,128)S(1)}, f32[1,18432]{1,0:T(1,128)}, u32[]{:S(2)}) copy-start(f32[1,18432]{1,0:T(1,128)} %mom_conv.1) | copy-start | bytes 221188
  0.6 71.9 %copy-start.1 = (f32[1,8192]{1,0:T(1,128)S(1)}, f32[1,8192]{1,0:T(1,128)}, u32[]{:S(2)}) copy-start(f32[1,8192]{1,0:T(1,128)} %mom_exp.1) | copy-start | bytes 98308

commit v5 on v4

--- a/solution.py
+++ b/solution.py
@@ -163,8 +163,8 @@
         else:
             acc[...] += part
 
-    def finish_forward(h):
-        pre = acc[...].astype(BF16)
+    def finish_forward(h, total):
+        pre = total.astype(BF16)
         hp[h] = pre
         ht[0, h] = nt(perm[...], jnp.maximum(pre, jnp.zeros((), BF16))).astype(BF16)
 
@@ -349,8 +349,8 @@
                 gacc[kind, n] = gacc[kind, n] + part
 
     for dy in range(3):
-        conv_taps(0, dy, dy == 0)
-    finish_forward(0)
+        w_copy(0, dy).wait()
+    finish_forward(0, nn(tap_row(xs, 0), wt[0, 0]) + nn(tap_row(xs, 1), wt[0, 1]) + nn(tap_row(xs, 2), wt[0, 2]))
     cot_copy.wait()
     we_copy.wait()
     pl.semaphore_wait(barrier, 22)
@@ -427,7 +427,7 @@
 
             @pl.when(p == 4)
             def _():
-                finish_forward(1)
+                finish_forward(1, acc[...])
 
         input_work(p)
         return carry
@@ -494,14 +494,21 @@
         drain(ref, send)
 
 
-def update_kernel(ig, fin_conv, fin_exp, mom_conv, mom_exp, ig_out, new_conv, new_exp, out_sem):
-    copy = pltpu.make_async_copy(ig, ig_out, out_sem)
-    copy.start()
-    for fin, mom, new in ((fin_conv, mom_conv, new_conv), (fin_exp, mom_exp, new_exp)):
+def update_kernel(
+    ig, fin_conv, fin_exp, mom_conv, mom_exp, ig_out, conv_out, exp_out, new_conv, new_exp, out_sem
+):
+    copies = [pltpu.make_async_copy(ig, ig_out, out_sem.at[0])]
+    copies[0].start()
+    for at, fin, mom, new, out in (
+        (1, fin_conv, mom_conv, new_conv, conv_out), (2, fin_exp, mom_exp, new_exp, exp_out),
+    ):
         n = fin.shape[1]
         for s in range(4):
             new[0:1, s * n : (s + 1) * n] = MOMENTUM * mom[0:1, s * n : (s + 1) * n] + fin[s : s + 1, :]
-    copy.wait()
+        copies.append(pltpu.make_async_copy(new, out, out_sem.at[at]))
+        copies[-1].start()
+    for copy in copies:
+        copy.wait()
 
 
 def body(inputs, cotangent, conv_weight, expand_weight, conv_momentum, expand_momentum):
@@ -563,8 +570,8 @@
             jax.ShapeDtypeStruct(expand_momentum.shape, F32),
         ),
         in_specs=[vmem_spec] * 5,
-        out_specs=(any_spec, vmem_spec, vmem_spec),
-        scratch_shapes=[dma],
+        out_specs=(any_spec,) * 3,
+        scratch_shapes=[vmem(conv_momentum.shape, F32), vmem(expand_momentum.shape, F32), dma((3,))],
         compiler_params=pltpu.CompilerParams(vmem_limit_bytes=8 * 1024 * 1024),
     )(input_grad, fin_conv, fin_exp, conv_momentum, expand_momentum)
 

time: 74.3 us -> 72 us (0.969)
  Pallas kernels: 73.5 us -> 71.2 us
    pallas_call x1, Pallas kernels: 71.9 us -> 70.2 us  [body(): pl.pallas_call(kernel, out_shape=(vmem(inputs.shape, BF16), vmem((4, 4608...]
where the time goes in v5:
time: 72 us; the launch traced here: 71.9 us
  Pallas kernels  71.2 us (99%)
    pallas_call x1, Pallas kernels, body(): pl.pallas_call(kernel, out_shape=(vmem(inputs.shape, BF16), vmem((4, 4608...  70.2 us

profile of v5, /device:TPU:1, one launch (start us, length us, event | category | flops | bytes accessed | tf_op | source)
XLA Modules:
  0.0 71.9 jit_solution(13200067557720800284)
XLA Ops:
  0.6 0.0 copy-start
  0.6 0.0 copy-start.1
  0.7 70.2 %shard_map.85 = (bf16[4,16,16,512]{3,2,1,0:T(8,128)(2,1)S(1)}, f32[4,4608]{1,0:T(4,128)S(1)}, f32[4,2048]{1,0:T(4,128)S(1)}) custom-call(bf16[4,16,16,512]{3,2,1,0:T(8,128)(2,1)} %x_hbm.1, bf16[1024,2048]{1,0:T(8,128)(2,1)} %bitcast.1, bf16[4608,512]{1,0:T(8,128)(2,1)} %w_hbm.1, bf16[512,2048]{1,0:T(8,128)(2,1)} %we_hbm.1), custom_call_target="tpu_custom_call" | custom-call | tf_op jit(solution)/shard_map/pallas_call | solution.py:521
  70.9 0.0 copy-done
  70.9 0.0 copy-done.1
  70.9 1.0 %shard_map.86 = (bf16[4,16,16,512]{3,2,1,0:T(8,128)(2,1)}, f32[1,18432]{1,0:T(1,128)}, f32[1,8192]{1,0:T(1,128)}) custom-call(bf16[4,16,16,512]{3,2,1,0:T(8,128)(2,1)S(1)} %get-tuple-element.6.ig, f32[4,4608]{1,0:T(4,128)S(1)} %get-tuple-element.7.fin_conv, f32[4,2048]{1,0:T(4,128)S(1)} %get-tuple-element.8.fin_exp, f32[1,18432]{1,0:T(1,128)S(1)} %copy-done, ...), custom_call_target="tpu_custom_call" | custom-call | tf_op jit(solution)/shard_map/pallas_call | solution.py:565
Async XLA Ops:
  0.6 70.2 %copy-start = (f32[1,18432]{1,0:T(1,128)S(1)}, f32[1,18432]{1,0:T(1,128)}, u32[]{:S(2)}) copy-start(f32[1,18432]{1,0:T(1,128)} %mom_conv.1) | copy-start | bytes 221188
  0.6 70.2 %copy-start.1 = (f32[1,8192]{1,0:T(1,128)S(1)}, f32[1,8192]{1,0:T(1,128)}, u32[]{:S(2)}) copy-start(f32[1,8192]{1,0:T(1,128)} %mom_exp.1) | copy-start | bytes 98308

commit v6 on v5

--- a/solution.py
+++ b/solution.py
@@ -86,9 +86,6 @@
         pl.semaphore_signal(barrier, inc=1, device_id={"inner": (i + d) % 16}, device_id_type=MESH)
         return carry
 
-    lax.fori_loop(1, 8, greet_outer, 0)
-    lax.fori_loop(1, 16, greet_inner, 0)
-
     def w_copy(h, dy):
         return pltpu.make_async_copy(
             w_hbm.at[pl.ds(dy * 1536, 1536), pl.ds(h * 256, 256)], wt.at[h, dy], w_sem.at[h, dy]
@@ -118,6 +115,9 @@
     for ty in range(3):
         for c in wn_copies(ty):
             c.start()
+
+    lax.fori_loop(1, 8, greet_outer, 0)
+    lax.fori_loop(1, 16, greet_inner, 0)
 
     row = lax.broadcasted_iota(jnp.int32, (256, 256), 0)
     col = lax.broadcasted_iota(jnp.int32, (256, 256), 1)

time: 72 us -> 71.6 us (level)
  no operation moved by 1% of the time
where the time goes in v6:
time: 71.6 us; the launch traced here: 71.4 us
  Pallas kernels  70.8 us (99%)
    pallas_call x1, Pallas kernels, body(): pl.pallas_call(kernel, out_shape=(vmem(inputs.shape, BF16), vmem((4, 4608...  69.8 us

profile of v6, /device:TPU:1, one launch (start us, length us, event | category | flops | bytes accessed | tf_op | source)
XLA Modules:
  0.0 71.4 jit_solution(4546541662964097504)
XLA Ops:
  0.6 0.0 copy-start
  0.6 0.0 copy-start.1
  0.7 69.8 %shard_map.85 = (bf16[4,16,16,512]{3,2,1,0:T(8,128)(2,1)S(1)}, f32[4,4608]{1,0:T(4,128)S(1)}, f32[4,2048]{1,0:T(4,128)S(1)}) custom-call(bf16[4,16,16,512]{3,2,1,0:T(8,128)(2,1)} %x_hbm.1, bf16[1024,2048]{1,0:T(8,128)(2,1)} %bitcast.1, bf16[4608,512]{1,0:T(8,128)(2,1)} %w_hbm.1, bf16[512,2048]{1,0:T(8,128)(2,1)} %we_hbm.1), custom_call_target="tpu_custom_call" | custom-call | tf_op jit(solution)/shard_map/pallas_call | solution.py:521
  70.4 0.0 copy-done
  70.4 0.0 copy-done.1
  70.4 1.0 %shard_map.86 = (bf16[4,16,16,512]{3,2,1,0:T(8,128)(2,1)}, f32[1,18432]{1,0:T(1,128)}, f32[1,8192]{1,0:T(1,128)}) custom-call(bf16[4,16,16,512]{3,2,1,0:T(8,128)(2,1)S(1)} %get-tuple-element.6.ig, f32[4,4608]{1,0:T(4,128)S(1)} %get-tuple-element.7.fin_conv, f32[4,2048]{1,0:T(4,128)S(1)} %get-tuple-element.8.fin_exp, f32[1,18432]{1,0:T(1,128)S(1)} %copy-done, ...), custom_call_target="tpu_custom_call" | custom-call | tf_op jit(solution)/shard_map/pallas_call | solution.py:565
Async XLA Ops:
  0.6 69.8 %copy-start = (f32[1,18432]{1,0:T(1,128)S(1)}, f32[1,18432]{1,0:T(1,128)}, u32[]{:S(2)}) copy-start(f32[1,18432]{1,0:T(1,128)} %mom_conv.1) | copy-start | bytes 221188
  0.6 69.8 %copy-start.1 = (f32[1,8192]{1,0:T(1,128)S(1)}, f32[1,8192]{1,0:T(1,128)}, u32[]{:S(2)}) copy-start(f32[1,8192]{1,0:T(1,128)} %mom_exp.1) | copy-start | bytes 98308
